TPU v7x, 32 devices: a whole 2x2x4 slice. The times are simulated.
32 devices in a mesh: gx: 8 (over z, y), gy: 4 (over x, core).
Axes of the slice: x: 2, y: 2, z: 4, core: 2. Of those that a mesh axis runs over, the one named last changes fastest.
Arguments:
- emb_table: float32 [65536, 128], P(('gx', 'gy')), may hold values from -0.6 to 0.6
- row_state: float32 [65536], P(('gx', 'gy')), may hold values from 1e-05 to 0.001
- pair_mask: int32 [8], P('gx'), may hold values from 0 to 3
- look_rows: int32 [196608], P(('gx', 'gy')), may hold values from 0 to 2047
- bag_sizes: int32 [32, 2048], P(('gx', 'gy')), may hold values from 1 to 12, 6144 in all within a row
- bag_owner: int32 [65536, 1], P(('gx', 'gy')), may hold values from 0 to 31, as said below
- bag_slot: int32 [65536], P(('gx', 'gy')), may hold values from 0 to 2047, as said below
- dense_vectors: float32 [4096, 128], P(('gx', 'gy')), may hold values from -3 to 3
- labels: float32 [4096], P(('gx', 'gy')), may hold values from 0 to 1
- top_weight: float32 [264, 1024], replicated, may hold values from -0.375 to 0.375
- out_weight: float32 [1024], replicated, may hold values from -0.1875 to 0.1875
Outputs:
- moved_table: float32 [65536, 128], P(('gx', 'gy'))
- moved_state: float32 [65536], P(('gx', 'gy'))
- top_grad: float32 [264, 1024], replicated
- out_grad: float32 [1024], replicated
Inputs may be any that keep to these rules, and one draw needn't show every extreme that they name: Device (g, y) trades with device (g, y xor pair_mask[g]); 0 keeps the block. `look_rows`: a row of the block that the device holds after the trade. `bag_sizes`: each device's sizes sum to 6144. `bag_owner`: among one device's 2048 bags every owner is named either never or exactly 128 times; each owner is named so by exactly half of the devices. `bag_slot`: sample times 16 plus feature; the bags that reach one owner name every one of its slots exactly once.
All inputs are finite; a program needn't handle non-finite values.
Results may differ from a plain program's by a relative error of at most 0.0003.
Values sent between devices are 32-bit elements; how exact they have to be, the bound alone decides.
No kernel may reach another device: no remote copies, remote signals or barrier semaphores. Data moves between devices by JAX's collectives and lax.ppermute only.
A program may use at most 64 MiB of HBM per device.

v0:
```python
import functools

import jax
import jax.numpy as jnp
from jax import lax
from jax.experimental import pallas as pl
from jax.experimental.pallas import tpu as pltpu
from jax.sharding import PartitionSpec as P


AXES = ("gx", "gy")
LANES = 128
TILE = 256
WINDOW = TILE + 8
learn_rate = 0.05
epsilon = 1e-08
HIGHEST = lax.Precision.HIGHEST
F32 = jnp.float32
BF16 = jnp.bfloat16
VMEM = pl.BlockSpec(memory_space=pltpu.VMEM)
SMEM = pl.BlockSpec(memory_space=pltpu.SMEM)
ANY = pl.BlockSpec(memory_space=pl.ANY)


def iota(shape, axis):
    return lax.broadcasted_iota(jnp.int32, shape, axis)


def ones_where(mask):
    return jnp.where(mask, 1.0, 0.0).astype(BF16)


def dot(a, b, **kw):
    return jnp.dot(a, b, preferred_element_type=F32, **kw)


def dot_t(a, b, **kw):
    return lax.dot_general(a, b, (((1,), (1,)), ((), ())), preferred_element_type=F32, **kw)


def split(x):
    high = x.astype(BF16)
    low = (x - high.astype(F32)).astype(BF16)
    return jnp.concatenate([high, low], axis=1)


def fold(x):
    half = x.shape[1] // 2
    return x[:, :half] + x[:, half:]


def prep_kernel(devices, capacity, features, look_ref, sizes_ref, owner_ref, slot_ref, dense_ref, labels_ref, meta_ref, slots_ref, bags_ref, told_ref):
    look_tiles = look_ref.shape[0]
    rows = sizes_ref.shape[0]
    samples = rows * LANES // features
    sizes = sizes_ref[...].astype(F32)
    owner = owner_ref[...]
    slot = slot_ref[...]
    lane_row, lane_col = iota((LANES, LANES), 0), iota((LANES, LANES), 1)
    upto = ones_where(lane_row <= lane_col)
    before = ones_where(lane_row < lane_col)
    every = jnp.ones((LANES, LANES), BF16)
    earlier = jnp.where(iota((rows, rows), 1) < iota((rows, rows), 0), 1.0, 0.0)
    sizes_b = sizes.astype(BF16)
    ends = dot(sizes_b, upto) + dot(earlier, dot(sizes_b, every), precision=HIGHEST)
    ends_i = ends.astype(jnp.int32)
    meta_ref[:look_tiles] = look_ref[...]
    meta_ref[look_tiles : look_tiles + rows] = (ends - sizes).astype(jnp.int32)
    meta_ref[look_tiles + rows : look_tiles + 2 * rows] = ends_i
    masks = [jnp.where(owner == d, 1.0, 0.0) for d in range(devices)]
    stack = jnp.concatenate(masks, axis=0).astype(BF16)
    ahead = dot(stack, before)
    total = dot(stack, every).astype(BF16)
    block = LANES // rows
    chain = ones_where((lane_row // rows == lane_col // rows) & (lane_col < lane_row))
    rank = jnp.zeros((rows, LANES), F32)
    for first in range(0, devices, block):
        part = slice(first * rows, (first + block) * rows)
        place = ahead[part] + dot(chain, total[part])
        for d in range(block):
            rank += masks[first + d] * place[d * rows : (d + 1) * rows]
    rank_i = rank.astype(jnp.int32)
    meta_ref[look_tiles + 2 * rows : look_tiles + 3 * rows] = owner * capacity + rank_i
    lane = iota((1, LANES), 1)
    starting = jnp.zeros((1, LANES), jnp.int32)
    for t in range(look_tiles * LANES // TILE):
        done = jnp.where(ends_i <= t * TILE, 1, 0)
        done = jnp.sum(jnp.sum(done, axis=0, keepdims=True), axis=1, keepdims=True)
        starting = jnp.where(lane == t, (done // 8) * 8, starting)
    meta_ref[look_tiles + 3 * rows :] = jnp.broadcast_to(starting, (8, LANES))
    where_to = (slot % features) * samples + slot // features
    high, low = (where_to // 64).astype(F32), (where_to % 64).astype(F32)
    found = jnp.zeros((5 * devices, LANES), F32)
    device_row = iota((devices, LANES), 0)
    across = iota((1, LANES), 1).astype(F32)
    for i in range(rows):
        mine = jnp.where(owner[i : i + 1] == device_row, 1.0, 0.0)
        left = jnp.concatenate(
            [mine * high[i : i + 1], mine * low[i : i + 1], mine, mine * float(i), mine * across], axis=0
        ).astype(BF16)
        found += dot_t(left, ones_where(rank_i[i : i + 1] == lane_row))
    found = [found[n * devices : (n + 1) * devices] for n in range(5)]
    slots_ref[...] = jnp.where(found[2] > 0.5, found[0] * 64 + found[1], -1.0).astype(jnp.int32)
    bags_ref[...] = jnp.where(found[2] > 0.5, found[3] * LANES + found[4], -1.0).astype(jnp.int32)
    told_ref[:samples] = dense_ref[...]
    told_ref[samples:] = jnp.broadcast_to(labels_ref[...], (8, LANES))


def column(row):
    return jnp.broadcast_to(row, (LANES, LANES)).T


def pool_kernel(look_tiles, rows, meta_s, meta_v, table, out, even, odd, pooled, first_k, last_k):
    bags = rows * LANES
    steps = look_tiles * LANES // TILE
    meta = meta_v[look_tiles : look_tiles + 2 * rows].astype(F32)
    for i in range(rows):
        at = slice(i * LANES, (i + 1) * LANES)
        first_k[at] = column(meta[i : i + 1])
        last_k[at] = column(meta[rows + i : rows + i + 1])
    first_k[bags:] = jnp.full((WINDOW, LANES), 1e9, F32)
    last_k[bags:] = jnp.full((WINDOW, LANES), -1.0, F32)
    pooled[...] = jnp.zeros_like(pooled)
    lane = iota((WINDOW, LANES), 1)

    def add_tile(t, source):
        window = pl.ds(pl.multiple_of(meta_s[look_tiles + 3 * rows, t], 8), WINDOW)
        first, last = first_k[window], last_k[window]
        parts = []
        for h in range(TILE // LANES):
            k = (lane + (t * TILE + h * LANES)).astype(F32)
            parts.append(ones_where((k >= first) & (k < last)))
        chosen = jnp.concatenate(parts, axis=1)
        pooled[window] += fold(dot(chosen, split(source[...])))

    def pick_tile(t, target):
        for c in range(TILE):
            target[c : c + 1] = table[pl.ds(meta_s[t * (TILE // LANES) + c // LANES, c % LANES], 1)]

    buffers = (even, odd)
    pick_tile(0, even)
    for t in range(1, steps):
        pick_tile(t, buffers[t % 2])
        add_tile(t - 1, buffers[(t - 1) % 2])
    add_tile(steps - 1, buffers[(steps - 1) % 2])

    for r in range(rows):
        for c in range(LANES):
            out[pl.ds(meta_s[look_tiles + 2 * rows + r, c], 1)] = pooled[r * LANES + c : r * LANES + c + 1]


def count_kernel(look_tiles, rows, meta_s, meta_v, out, total):
    i = pl.program_id(0)
    per = TILE // LANES
    start_row = look_tiles + i * per
    lowest = meta_s[start_row, 0]
    highest = meta_s[start_row + rows + per - 1, LANES - 1]
    starts = jnp.concatenate([meta_v[pl.ds(start_row + h, 1)] for h in range(per)], axis=1)
    ends = jnp.concatenate([meta_v[pl.ds(start_row + rows + h, 1)] for h in range(per)], axis=1)
    total[...] = jnp.zeros_like(total)

    @pl.loop(lowest // TILE, (highest + TILE - 1) // TILE)
    def _(c):
        look = jnp.concatenate([meta_v[pl.ds(c * per + h, 1)] for h in range(per)], axis=1)
        k = iota((TILE, TILE), 0) + c * TILE
        member = ones_where((k >= starts) & (k < ends))
        picked = ones_where(iota((total.shape[0], TILE), 0) == look)
        total[...] += dot(picked, member)

    out[...] = total[...].astype(BF16)


def pairs_of(features):
    return [(i, j) for i in range(features + 1) for j in range(i + 1, features + 1)]


def tile_of(dense, vectors, samples, features, at):
    return [dense[pl.ds(at, 8)]] + [vectors[pl.ds(f * samples + at, 8)] for f in range(features)]


def scatter_rows(places, source, capacity, blocks, target):
    for s in range(places.shape[0]):

        @pl.when(places[s, 0] >= 0)
        def _():
            part = blocks.at[pl.ds(pl.multiple_of(source(s) * capacity, 8), capacity)]
            for j in range(capacity):
                target[pl.ds(places[s, j], 1)] = part[j : j + 1]


def gram_kernel(features, capacity, slots, source, got, dense, vectors, pairs, more):
    samples = dense.shape[0]
    scatter_rows(slots, lambda s: source[s], capacity, got, vectors)
    lane = iota((8, LANES), 1)

    @pl.loop(0, samples // 8)
    def _(t):
        at = pl.multiple_of(t * 8, 8)
        each = tile_of(dense, vectors, samples, features, at)
        tiles = [jnp.zeros((8, LANES), F32) for _ in range(2)]
        for p, (i, j) in enumerate(pairs_of(features)):
            inner = jnp.sum(each[i] * each[j], axis=1, keepdims=True)
            tiles[p // LANES] = jnp.where(lane == p % LANES, inner, tiles[p // LANES])
        pairs[pl.ds(at, 8)] = tiles[0]
        more[pl.ds(at, 8)] = tiles[1]

    pairs[samples:] = more[...].T[: pairs.shape[0] - samples]


def halves_of(x):
    high = x.astype(BF16)
    return high, (x - high.astype(F32)).astype(BF16)


def weight_kernel(weight, right, left):
    inter = weight.shape[0]
    dense_h, dense_l = halves_of(weight[:LANES])
    pairs_h, pairs_l = halves_of(weight[LANES : 2 * LANES])
    rest_h, rest_l = halves_of(weight[2 * LANES :])
    rest_h, rest_l = rest_h.astype(F32), rest_l.astype(F32)
    hidden = weight.shape[1]
    gap = jnp.zeros((LANES - 3 * (inter - 2 * LANES), hidden), F32)
    rest = jnp.concatenate([rest_h, rest_l, rest_h, gap], axis=0).astype(BF16)
    right[...] = jnp.concatenate([dense_h, pairs_h, dense_l, pairs_l, dense_h, pairs_h, rest], axis=0)
    gap = jnp.zeros((3 * LANES - inter, hidden), F32)
    tail_h = jnp.concatenate([rest_h, gap], axis=0).astype(BF16)
    tail_l = jnp.concatenate([rest_l, gap], axis=0).astype(BF16)
    for n, (head, tail) in enumerate(((pairs_h, tail_h), (pairs_l, tail_l), (pairs_h, tail_h))):
        left[:, n * hidden : (n + 1) * hidden] = jnp.concatenate([head, tail], axis=0)


def inputs_of(dense, told):
    samples = dense.shape[0]
    dense_h, dense_l = halves_of(dense)
    pairs_h, pairs_l = halves_of(told[:samples])
    tail = told[samples:]
    tail_h = tail.astype(BF16).astype(F32)
    gap = jnp.zeros((LANES - 3 * tail.shape[0], samples), F32)
    rest = jnp.concatenate([tail_h, tail_h, tail - tail_h, gap], axis=0).T.astype(BF16)
    return jnp.concatenate([dense_h, pairs_h, dense_h, pairs_h, dense_l, pairs_l, rest], axis=1)


def forward(x, labels, weight, out_weight):
    pre = dot(x, weight)
    gate = 1.0 / (1.0 + jnp.exp(-pre))
    hidden = pre * gate
    logits = jnp.sum(hidden * out_weight, axis=1, keepdims=True)
    d_logits = 1.0 / (1.0 + jnp.exp(-logits)) - labels
    d_pre = d_logits * out_weight * (gate + hidden * (1.0 - gate))
    return hidden, d_logits, d_pre


def back_kernel(features, capacity, slots, dense, vectors, pairs, labels, weight, left, out_weight, back, d_vectors, d_pairs, ready, sent):
    devices = slots.shape[0]
    samples = dense.shape[0]
    x = inputs_of(dense[...], pairs[...])
    _, _, d_pre = forward(x, column(labels[...])[:, :1], weight[...], out_weight[...])
    high, low = halves_of(d_pre)
    d_pairs[...] = dot_t(jnp.concatenate([high, high, low], axis=1), left[...])

    @pl.loop(0, samples // 8)
    def _(t):
        at = pl.multiple_of(t * 8, 8)
        each = tile_of(dense, vectors, samples, features, at)
        slopes = d_pairs[pl.ds(at, 8)]
        sums = [None] * (features + 1)
        for p, (i, j) in enumerate(pairs_of(features)):
            slope = jnp.broadcast_to(slopes[:, p : p + 1], (8, LANES))
            if i > 0:
                sums[i] = slope * each[j] if sums[i] is None else sums[i] + slope * each[j]
            sums[j] = slope * each[i] if sums[j] is None else sums[j] + slope * each[i]
        for f in range(features):
            d_vectors[pl.ds(f * samples + at, 8)] = sums[f + 1]

    def copy(s):
        part = pl.ds(pl.multiple_of(s * capacity, 8), capacity)
        return pltpu.make_async_copy(ready.at[part], back.at[part], sent.at[s])

    for s in range(devices):

        @pl.when(slots[s, 0] >= 0)
        def _(s=s):
            for j in range(s * capacity, (s + 1) * capacity):
                ready[j : j + 1] = d_vectors[pl.ds(slots[s, j - s * capacity], 1)]
            copy(s).start()

    @pl.loop(0, devices)
    def _(s):
        @pl.when(slots[s, 0] >= 0)
        def _():
            copy(s).wait()


def pack_kernel(*refs):
    size = refs[0].shape[0]
    for n, ref in enumerate(refs[:-1]):
        refs[-1][n * size : (n + 1) * size] = ref[...]


def top_kernel(parts, *refs):
    dense_refs, pairs_refs = refs[:parts], refs[parts : 2 * parts]
    weight, out_weight, grad, dense_all, pairs_all = refs[2 * parts :]
    size = dense_refs[0].shape[0]
    inter = grad.shape[0] - 8
    block = LANES + inter - 2 * LANES
    for n in range(parts):
        dense_all[n * size : (n + 1) * size] = dense_refs[n][...]
        pairs_all[n * size : (n + 1) * size] = pairs_refs[n][...]
    grad[...] = jnp.zeros_like(grad)

    @pl.loop(0, parts)
    def _(n):
        xs, labels, columns = [], [], []
        for m in range(size // block):
            at = pl.ds(pl.multiple_of(n * size + m * block, 8), block)
            rows, told = dense_all[at], pairs_all[at]
            dense = rows[:LANES]
            xs.append(inputs_of(dense, told))
            labels.append(column(rows[LANES : LANES + 1])[:, :1])
            columns.append(jnp.concatenate([dense.T, told[:LANES].T, told[LANES:], jnp.zeros((8, LANES), F32)], axis=0))
        hidden, d_logits, d_pre = forward(
            jnp.concatenate(xs, axis=0), jnp.concatenate(labels, axis=0), weight[...], out_weight[...]
        )
        x_high, x_low = halves_of(jnp.concatenate(columns, axis=1))
        d_high, d_low = halves_of(d_pre)
        grad[...] += dot(
            jnp.concatenate([x_high, x_high, x_low], axis=1), jnp.concatenate([d_high, d_low, d_high], axis=0)
        )
        grad[inter:] += jnp.broadcast_to(jnp.sum(hidden * d_logits, axis=0, keepdims=True), (8, grad.shape[1]))


def update_kernel(capacity, chunks, bags_s, came, counts, table, state, new_table, new_state, grads):
    scatter_rows(bags_s, lambda s: s, capacity, came, grads)
    parts = split(grads[...])
    width = grads.shape[1]
    size = counts.shape[0] // chunks
    for n in range(chunks):
        row_grad = fold(dot(counts[n * size : (n + 1) * size], parts))
        for j in range(size // LANES):
            tile = n * (size // LANES) + j
            at = slice(tile * LANES, (tile + 1) * LANES)
            grad = row_grad[j * LANES : (j + 1) * LANES]
            moved = column(state[tile : tile + 1]) + jnp.sum(grad * grad, axis=1, keepdims=True) / width
            new_table[at] = table[at] - learn_rate * grad / (jnp.sqrt(moved) + epsilon)
            new_state[tile : tile + 1] = moved.T[:1]


def trade(values, pair_value):
    result = values
    for bit in range(lax.axis_size("gy").bit_length() - 1):
        route = [(y, y ^ 1 << bit) for y in range(lax.axis_size("gy"))]
        partner = jax.tree.map(lambda x: lax.ppermute(x, "gy", route), result)
        flipped = jnp.bitwise_and(jnp.right_shift(pair_value, bit), 1) == 1
        result = jax.tree.map(functools.partial(jnp.where, flipped), partner, result)
    return result


def exchange(x):
    return lax.all_to_all(x, AXES, split_axis=0, concat_axis=0, tiled=True)


def in_vmem(value):
    return pltpu.with_memory_space_constraint(value, pltpu.VMEM)


def swap(value, offset):
    devices = lax.axis_size("gx") * lax.axis_size("gy")
    return lax.ppermute(value, AXES, [(d, d ^ offset) for d in range(devices)])


def gather_near(value):
    bits = (lax.axis_size("gx") * lax.axis_size("gy")).bit_length() - 1
    far = [value] + [swap(value, k << bits - 2) for k in range(1, 4)]
    value = pl.pallas_call(
        pack_kernel,
        out_shape=jax.ShapeDtypeStruct((4 * value.shape[0], value.shape[1]), value.dtype),
        in_specs=[VMEM] * 4,
        out_specs=VMEM,
    )(*far)
    return [value] + [swap(value, k << bits - 4) for k in range(1, 4)]


def sum_rest(value):
    bits = (lax.axis_size("gx") * lax.axis_size("gy")).bit_length() - 1
    for bit in range(bits - 4):
        value = value + swap(value, 1 << bit)
    return value


def on_device(
    emb_table, row_state, pair_mask, look_rows, bag_sizes, bag_owner, bag_slot, dense_vectors, labels, top_weight, out_weight
):
    groups_y = lax.axis_size("gy")
    devices = lax.axis_size("gx") * groups_y
    table_rows, width = emb_table.shape
    bags = bag_slot.shape[0]
    capacity = 2 * bags // devices
    samples = dense_vectors.shape[0]
    features = bags // samples
    look_tiles, rows = look_rows.shape[0] // LANES, bags // LANES
    inter, hidden = top_weight.shape
    pair_value = pair_mask[0]
    shape = jax.ShapeDtypeStruct

    tail = inter - 2 * LANES
    meta, slots, places, dense_told = pl.pallas_call(
        functools.partial(prep_kernel, devices, capacity, features),
        out_shape=(
            shape((look_tiles + 3 * rows + 8, LANES), jnp.int32),
            shape((devices, LANES), jnp.int32),
            shape((devices, LANES), jnp.int32),
            shape((samples + tail, width), F32),
        ),
        in_specs=[VMEM] * 6,
        out_specs=(VMEM,) * 4,
        name="prep",
    )(
        look_rows.reshape(look_tiles, LANES),
        bag_sizes.reshape(rows, LANES),
        bag_owner.reshape(rows, LANES),
        bag_slot.reshape(rows, LANES),
        dense_vectors,
        labels.reshape(1, samples),
    )
    traded_meta = trade(meta, pair_value)
    told = jnp.stack([slots[:, :capacity], jnp.full((devices, capacity), pair_value)], axis=1)
    told = exchange(told)
    got_slots = told[:, 0]
    source = jnp.bitwise_xor(jnp.arange(devices, dtype=jnp.int32), told[:, 1, 0])

    sent = pl.pallas_call(
        functools.partial(pool_kernel, look_tiles, rows),
        out_shape=shape((devices * capacity, width), F32),
        in_specs=[SMEM, VMEM, VMEM],
        out_specs=VMEM,
        scratch_shapes=[
            pltpu.VMEM((TILE, width), F32),
            pltpu.VMEM((TILE, width), F32),
            pltpu.VMEM((bags + WINDOW, width), F32),
            pltpu.VMEM((bags + WINDOW, LANES), F32),
            pltpu.VMEM((bags + WINDOW, LANES), F32),
        ],
        name="pool",
    )(traded_meta, traded_meta, emb_table)
    dense_told, sent = lax.optimization_barrier((dense_told, sent))
    got = exchange(sent.reshape(devices, capacity, width))
    got = got.reshape(devices * capacity, width)

    held_table = trade(emb_table, pair_value)
    held_state = trade(row_state.reshape(-1, LANES), pair_value)
    counts = pl.pallas_call(
        functools.partial(count_kernel, look_tiles, rows),
        out_shape=shape((table_rows, bags), BF16),
        grid=(bags // TILE,),
        in_specs=[SMEM, VMEM],
        out_specs=pl.BlockSpec((table_rows, TILE), lambda i: (0, i)),
        scratch_shapes=[pltpu.VMEM((table_rows, TILE), F32)],
        name="count",
    )(meta, meta)

    right, left = pl.pallas_call(
        weight_kernel,
        out_shape=(shape((7 * LANES, hidden), BF16), shape((2 * LANES, 3 * hidden), BF16)),
        in_specs=[VMEM],
        out_specs=(VMEM, VMEM),
        name="weights",
    )(top_weight)
    out_row = out_weight.reshape(1, hidden)
    block_scratch = [pltpu.VMEM((devices * capacity, width), F32), pltpu.SemaphoreType.DMA((devices,))]
    vectors, pairs = pl.pallas_call(
        functools.partial(gram_kernel, features, capacity),
        out_shape=(shape((bags, width), F32), shape((samples + tail, LANES), F32)),
        in_specs=[SMEM, SMEM, VMEM, VMEM],
        out_specs=(VMEM, VMEM),
        scratch_shapes=[pltpu.VMEM((samples, LANES), F32)],
        compiler_params=pltpu.CompilerParams(vmem_limit_bytes=16 << 20),
        name="gram",
    )(got_slots, source, in_vmem(got), dense_vectors)
    near_dense = gather_near(dense_told)
    near_pairs = gather_near(pairs)

    back = pl.pallas_call(
        functools.partial(back_kernel, features, capacity),
        out_shape=shape((devices * capacity, width), F32),
        in_specs=[SMEM] + [VMEM] * 7,
        out_specs=ANY,
        scratch_shapes=[pltpu.VMEM((bags, width), F32), pltpu.VMEM((samples, 2 * LANES), F32)] + block_scratch,
        name="back",
    )(got_slots, dense_vectors, vectors, pairs, labels.reshape(1, samples), right, left, out_row)
    came = exchange(back.reshape(devices, capacity, width))
    came = came.reshape(devices * capacity, width)

    gathered = len(near_dense) * near_dense[0].shape[0]
    local = pl.pallas_call(
        functools.partial(top_kernel, len(near_dense)),
        out_shape=shape((inter + 8, hidden), F32),
        in_specs=[VMEM] * (2 * len(near_dense) + 2),
        out_specs=VMEM,
        scratch_shapes=[pltpu.VMEM((gathered, LANES), F32)] * 2,
        name="top",
    )(*near_dense, *near_pairs, right, out_row)
    summed = sum_rest(local)

    chunks = 4
    update = pl.pallas_call(
        functools.partial(update_kernel, capacity, chunks),
        out_shape=(shape((table_rows, width), F32), shape((table_rows // LANES, LANES), F32)),
        in_specs=[SMEM] + [VMEM] * 4,
        out_specs=(VMEM, VMEM),
        scratch_shapes=[pltpu.VMEM((bags, width), F32)],
        compiler_params=pltpu.CompilerParams(vmem_limit_bytes=24 << 20),
        name="update",
    )
    new_table, new_state = update(places, in_vmem(came), in_vmem(counts), in_vmem(held_table), held_state)
    return new_table, new_state.reshape(-1), summed[:inter], summed[inter]


def solution(mesh):
    both = P(AXES)
    in_specs = (P(AXES, None), both, P("gx"), both, P(AXES, None), P(AXES, None), both, P(AXES, None), both, P(), P())
    out_specs = (P(AXES, None), both, P(), P())
    return jax.shard_map(on_device, mesh=mesh, in_specs=in_specs, out_specs=out_specs, check_vma=False)
```

profile of v0, /device:TPU:0, one launch (start us, length us, event | category | flops | bytes accessed | tf_op | source)
XLA Modules:
  0.0 261.0 jit_solution(5752489169546185996)
XLA Ops:
  0.6 2.6 %prep.1 = (s32[104,128]{1,0:T(8,128)}, s32[32,128]{1,0:T(8,128)}, s32[32,128]{1,0:T(8,128)}, f32[136,128]{1,0:T(8,128)}) custom-call(s32[48,128]{1,0:T(8,128)} %bitcast.33, s32[16,128]{1,0:T(8,128)} %bitcast.37, s32[16,128]{1,0:T(8,128)} %bitcast.38, s32[16,128]{1,0:T(8,128)} %bitcast.39, f32[128,128]{1,0:T(8,128)} %dense.3, f32[1,128]{1,0:T(1,128)} %bitcast.41), custom_call_target="tpu_custom_call" | custom-call | tf_op jit(solution)/shard_map/prep/pallas_call | solution.py:406
  4.9 0.8 broadcast_select_fusion.2
  5.7 2.8 %collective-permute-start.1 = (s32[104,128]{1,0:T(8,128)S(1)}, s32[104,128]{1,0:T(8,128)S(1)}, u32[]{:S(2)}, u32[]{:S(2)}) collective-permute-start(s32[104,128]{1,0:T(8,128)S(1)} %broadcast_select_fusion.2), channel_id=1, source_target_pairs={{0,2},{1,3},{2,0},{3,1},{4,6},{5,7},{6,4},{7,5},{8,10},{9,11},{10,... | collective-permute-start | bytes 159752 | tf_op jit(solution)/shard_map/ppermute | solution.py:352
  8.5 1.3 stack.7.clone
  9.8 4.2 %all-to-all-start = ((s32[32,2,128]{2,1,0:T(2,128)}), s32[32,2,128]{2,1,0:T(2,128)S(1)}, u32[]{:S(2)}, u32[]{:S(2)}) async-start(s32[32,2,128]{2,1,0:T(2,128)} %stack.7.clone), calls=%async_computation | async-start | bytes 65536 | tf_op jit(solution)/shard_map/all_to_all | solution.py:359
  14.0 0.6 broadcast_select_fusion.3.meta_s.meta_v
  14.7 9.4 %pool.1 = f32[4096,128]{1,0:T(8,128)} custom-call(s32[104,128]{1,0:T(8,128)} %broadcast_select_fusion.3.meta_s.meta_v, s32[104,128]{1,0:T(8,128)} %broadcast_select_fusion.3.meta_s.meta_v, f32[2048,128]{1,0:T(8,128)} %table.1), custom_call_target="tpu_custom_call" | custom-call | tf_op jit(solution)/shard_map/pool/pallas_call | solution.py:431
  24.1 5.8 %all-to-all-start.1 = ((f32[32,128,128]{2,1,0:T(8,128)}), f32[32,128,128]{2,1,0:T(8,128)S(1)}, u32[]{:S(2)}, u32[]{:S(2)}) async-start(f32[32,128,128]{2,1,0:T(8,128)} %bitcast.30), calls=%async_computation.1 | async-start | bytes 4194304 | tf_op jit(solution)/shard_map/all_to_all | solution.py:359
  30.0 3.3 %weights.1 = (bf16[896,1024]{1,0:T(8,128)(2,1)}, bf16[256,3072]{1,0:T(8,128)(2,1)}) custom-call(f32[264,1024]{1,0:T(8,128)} %weight.1), custom_call_target="tpu_custom_call" | custom-call | tf_op jit(solution)/shard_map/weights/pallas_call | solution.py:461
  33.3 0.7 slice_reduce_fusion
  34.0 44.7 %all-to-all-done.1 = f32[32,128,128]{2,1,0:T(8,128)S(1)} async-done(((f32[32,128,128]{2,1,0:T(8,128)}), f32[32,128,128]{2,1,0:T(8,128)S(1)}, u32[]{:S(2)}, u32[]{:S(2)}) %all-to-all-start.1) | async-done | bytes 2097184 | tf_op jit(solution)/shard_map/all_to_all | solution.py:359
  78.7 5.7 %gram.1 = (f32[2048,128]{1,0:T(8,128)S(1)}, f32[136,128]{1,0:T(8,128)S(1)}) custom-call(s32[32,128]{1,0:T(8,128)S(1)} %bitcast.28, s32[32]{0:T(128)S(1)} %iota_xor_fusion.source, f32[4096,128]{1,0:T(8,128)S(1)} %bitcast.27, f32[128,128]{1,0:T(8,128)S(1)} %copy-done.2), custom_call_target="tpu_custom_call" | custom-call | tf_op jit(solution)/shard_map/gram/pallas_call | solution.py:470
  84.4 1.0 copy-done.1
  85.4 0.6 copy-done.3
  86.1 11.0 %back.1 = f32[4096,128]{1,0:T(8,128)} custom-call(s32[32,128]{1,0:T(8,128)} %bitcast.29, f32[128,128]{1,0:T(8,128)} %dense.3, f32[2048,128]{1,0:T(8,128)} %copy-done.1, f32[136,128]{1,0:T(8,128)} %copy-done.3, f32[1,128]{1,0:T(1,128)} %bitcast.42, bf16[896,1024]{1,0:T(8,128)(2,1)} %get-tuple-element.23.weight.refs_8_, ...), custom_call_target="tpu_custom_call" | custom-call | tf_op jit(solution)/shard_map/back/pallas_call | solution.py:482
  97.1 4.1 %all-to-all-start.2 = ((f32[32,128,128]{2,1,0:T(8,128)}), f32[32,128,128]{2,1,0:T(8,128)S(1)}, u32[]{:S(2)}, u32[]{:S(2)}) async-start(f32[32,128,128]{2,1,0:T(8,128)} %bitcast.31), calls=%async_computation.2 | async-start | bytes 4194304 | tf_op jit(solution)/shard_map/all_to_all | solution.py:359
  101.5 3.5 %collective-permute-start.8 = (f32[136,128]{1,0:T(8,128)S(1)}, f32[136,128]{1,0:T(8,128)S(1)}, u32[]{:S(2)}, u32[]{:S(2)}) collective-permute-start(f32[136,128]{1,0:T(8,128)S(1)} %copy-done.13), channel_id=1, source_target_pairs={{0,24},{1,25},{2,26},{3,27},{4,28},{5,29},{6,30},{7,31},{8,16},{9,... | collective-permute-start | bytes 208904 | tf_op jit(solution)/shard_map/ppermute | solution.py:368
  105.0 0.9 collective-permute-start.6
  105.9 35.8 %collective-permute-done.8.refs_3_ = f32[136,128]{1,0:T(8,128)S(1)} collective-permute-done((f32[136,128]{1,0:T(8,128)S(1)}, f32[136,128]{1,0:T(8,128)S(1)}, u32[]{:S(2)}, u32[]{:S(2)}) %collective-permute-start.8) | collective-permute-done | bytes 69664 | tf_op jit(solution)/shard_map/ppermute | solution.py:368
  141.7 14.2 %collective-permute-done.7.refs_2_ = f32[136,128]{1,0:T(8,128)S(1)} collective-permute-done((f32[136,128]{1,0:T(8,128)S(1)}, f32[136,128]{1,0:T(8,128)S(1)}, u32[]{:S(2)}, u32[]{:S(2)}) %collective-permute-start.7) | collective-permute-done | bytes 69664 | tf_op jit(solution)/shard_map/ppermute | solution.py:368
  155.9 0.6 copy-done.17
  156.5 0.6 copy-done.19
  157.2 1.7 shard_map.138.refs_0_
  158.9 2.4 collective-permute-start.11
  161.3 0.6 collective-permute-start.10
  161.9 1.1 broadcast_select_fusion
  163.5 3.1 %collective-permute-start.14 = (f32[136,128]{1,0:T(8,128)S(1)}, f32[136,128]{1,0:T(8,128)S(1)}, u32[]{:S(2)}, u32[]{:S(2)}) collective-permute-start(f32[136,128]{1,0:T(8,128)S(1)} %copy-done.4), channel_id=1, source_target_pairs={{0,24},{1,25},{2,26},{3,27},{4,28},{5,29},{6,30},{7,31},{8,16},{9,... | collective-permute-start | bytes 208904 | tf_op jit(solution)/shard_map/ppermute | solution.py:368
  166.6 3.1 %collective-permute-done.14.refs_3_ = f32[136,128]{1,0:T(8,128)S(1)} collective-permute-done((f32[136,128]{1,0:T(8,128)S(1)}, f32[136,128]{1,0:T(8,128)S(1)}, u32[]{:S(2)}, u32[]{:S(2)}) %collective-permute-start.14) | collective-permute-done | bytes 69664 | tf_op jit(solution)/shard_map/ppermute | solution.py:368
  169.7 2.3 collective-permute-done.13.refs_2_
  172.0 1.4 collective-permute-start.9
  173.4 0.6 collective-permute-done.12.refs_1_
  174.0 0.6 copy-done.18
  174.6 1.7 shard_map.139.refs_4_
  176.3 2.4 collective-permute-start.17
  178.8 0.6 collective-permute-start.16
  179.8 18.1 %collective-permute-done.9.refs_1_ = f32[544,128]{1,0:T(8,128)S(1)} collective-permute-done((f32[544,128]{1,0:T(8,128)S(1)}, f32[544,128]{1,0:T(8,128)S(1)}, u32[]{:S(2)}, u32[]{:S(2)}) %collective-permute-start.9) | collective-permute-done | bytes 278560 | tf_op jit(solution)/shard_map/ppermute | solution.py:368
  197.9 6.0 %collective-permute-done.17.refs_7_ = f32[544,128]{1,0:T(8,128)S(1)} collective-permute-done((f32[544,128]{1,0:T(8,128)}, f32[544,128]{1,0:T(8,128)S(1)}, u32[]{:S(2)}, u32[]{:S(2)}) %collective-permute-start.17) | collective-permute-done | bytes 278560 | tf_op jit(solution)/shard_map/ppermute | solution.py:368
  204.0 4.6 %collective-permute-done.15.refs_5_ = f32[544,128]{1,0:T(8,128)} collective-permute-done((f32[544,128]{1,0:T(8,128)}, f32[544,128]{1,0:T(8,128)}, u32[]{:S(2)}, u32[]{:S(2)}) %collective-permute-start.15) | collective-permute-done | bytes 278560 | tf_op jit(solution)/shard_map/ppermute | solution.py:368
  208.6 15.4 %top.1 = f32[272,1024]{1,0:T(8,128)} custom-call(f32[544,128]{1,0:T(8,128)} %shard_map.138.refs_0_, f32[544,128]{1,0:T(8,128)} %copy-done.10, f32[544,128]{1,0:T(8,128)} %collective-permute-done.10.refs_2_, f32[544,128]{1,0:T(8,128)} %collective-permute-done.11.refs_3_, f32[544,128]{1,0:T(8,128)} %shard_map.139.refs_4_, ...), custom_call_target="tpu_custom_call" | custom-call | tf_op jit(solution)/shard_map/top/pallas_call | solution.py:494
  224.5 2.6 collective-permute-done.4
  227.1 1.5 collective-permute-start.5
  228.6 18.5 %count.1.counts = bf16[2048,2048]{1,0:T(8,128)(2,1)} custom-call(s32[104,128]{1,0:T(8,128)} %get-tuple-element.19.meta_s.meta_v, s32[104,128]{1,0:T(8,128)} %get-tuple-element.19.meta_s.meta_v), custom_call_target="tpu_custom_call" | custom-call | tf_op jit(solution)/shard_map/count/pallas_call | solution.py:451
  247.1 1.4 broadcast_select_fusion.1.table
  248.7 1.4 add.5
  250.1 0.6 slice.19
  250.7 1.1 slice.18
  251.8 3.4 %copy-done = bf16[2048,2048]{1,0:T(8,128)(2,1)S(1)} copy-done((bf16[2048,2048]{1,0:T(8,128)(2,1)S(1)}, bf16[2048,2048]{1,0:T(8,128)(2,1)}, u32[]{:S(2)}) %copy-start) | copy-done | bytes 8388632
  255.2 5.8 %update.1 = (f32[2048,128]{1,0:T(8,128)}, f32[16,128]{1,0:T(8,128)}) custom-call(s32[32,128]{1,0:T(8,128)S(1)} %copy-done.6, f32[4096,128]{1,0:T(8,128)S(1)} %bitcast.26, bf16[2048,2048]{1,0:T(8,128)(2,1)S(1)} %copy-done, f32[2048,128]{1,0:T(8,128)S(1)} %broadcast_select_fusion.1.table, f32[16,128]{1,0:T(8,128)S(1)} %broadcast_select_fusion.5.state), custom_call_target="tpu_custom_call" | custom-call | tf_op jit(solution)/shard_map/update/pallas_call | solution.py:514
  (61 shorter events, 2.9 us)
Async XLA Ops:
  3.3 1.6 collective-permute-start
  5.7 8.4 %collective-permute-start.1 = (s32[104,128]{1,0:T(8,128)S(1)}, s32[104,128]{1,0:T(8,128)S(1)}, u32[]{:S(2)}, u32[]{:S(2)}) collective-permute-start(s32[104,128]{1,0:T(8,128)S(1)} %broadcast_select_fusion.2), channel_id=1, source_target_pairs={{0,2},{1,3},{2,0},{3,1},{4,6},{5,7},{6,4},{7,5},{8,10},{9,11},{10,... | collective-permute-start | bytes 159752 | tf_op jit(solution)/shard_map/ppermute | solution.py:352
  9.8 14.3 %all-to-all-start = ((s32[32,2,128]{2,1,0:T(2,128)}), s32[32,2,128]{2,1,0:T(2,128)S(1)}, u32[]{:S(2)}, u32[]{:S(2)}) async-start(s32[32,2,128]{2,1,0:T(2,128)} %stack.7.clone), calls=%async_computation | async-start | bytes 65536 | tf_op jit(solution)/shard_map/all_to_all | solution.py:359
  24.1 54.6 %copy-start.2 = (f32[128,128]{1,0:T(8,128)S(1)}, f32[128,128]{1,0:T(8,128)}, u32[]{:S(2)}) copy-start(f32[128,128]{1,0:T(8,128)} %dense.3) | copy-start | bytes 196612
  24.1 54.6 %all-to-all-start.1 = ((f32[32,128,128]{2,1,0:T(8,128)}), f32[32,128,128]{2,1,0:T(8,128)S(1)}, u32[]{:S(2)}, u32[]{:S(2)}) async-start(f32[32,128,128]{2,1,0:T(8,128)} %bitcast.30), calls=%async_computation.1 | async-start | bytes 4194304 | tf_op jit(solution)/shard_map/all_to_all | solution.py:359
  33.3 52.8 %copy-start.5 = (s32[32,1,128]{2,1,0:T(1,128)}, s32[32,1,128]{2,1,0:T(1,128)S(1)}, u32[]{:S(2)}) copy-start(s32[32,1,128]{2,1,0:T(1,128)S(1)} %slice.16) | copy-start | bytes 49156
  84.4 1.0 copy-start.1
  85.4 0.6 copy-start.3
  97.1 4.1 %copy-start.8 = (f32[2048,128]{1,0:T(8,128)S(1)}, f32[2048,128]{1,0:T(8,128)}, u32[]{:S(2)}) copy-start(f32[2048,128]{1,0:T(8,128)} %table.1) | copy-start | bytes 3145732
  97.1 4.5 %copy-start.13 = (f32[136,128]{1,0:T(8,128)S(1)}, f32[136,128]{1,0:T(8,128)}, u32[]{:S(2)}) copy-start(f32[136,128]{1,0:T(8,128)} %get-tuple-element.27.refs_0_) | copy-start | bytes 208900
  97.1 154.7 %all-to-all-start.2 = ((f32[32,128,128]{2,1,0:T(8,128)}), f32[32,128,128]{2,1,0:T(8,128)S(1)}, u32[]{:S(2)}, u32[]{:S(2)}) async-start(f32[32,128,128]{2,1,0:T(8,128)} %bitcast.31), calls=%async_computation.2 | async-start | bytes 4194304 | tf_op jit(solution)/shard_map/all_to_all | solution.py:359
  101.2 62.3 %copy-start.4 = (f32[136,128]{1,0:T(8,128)S(1)}, f32[136,128]{1,0:T(8,128)}, u32[]{:S(2)}) copy-start(f32[136,128]{1,0:T(8,128)} %copy-done.3) | copy-start | bytes 208900
  101.2 60.7 %collective-permute-start.2 = (f32[2048,128]{1,0:T(8,128)S(1)}, f32[2048,128]{1,0:T(8,128)}, u32[]{:S(2)}, u32[]{:S(2)}) collective-permute-start(f32[2048,128]{1,0:T(8,128)S(1)} %copy-done.8), channel_id=1, source_target_pairs={{0,1},{1,0},{2,3},{3,2},{4,5},{5,4},{6,7},{7,6},{8,9},{9,8},{10,11... | collective-permute-start | bytes 3145736 | tf_op jit(solution)/shard_map/ppermute | solution.py:352
  101.5 40.2 %collective-permute-start.8 = (f32[136,128]{1,0:T(8,128)S(1)}, f32[136,128]{1,0:T(8,128)S(1)}, u32[]{:S(2)}, u32[]{:S(2)}) collective-permute-start(f32[136,128]{1,0:T(8,128)S(1)} %copy-done.13), channel_id=1, source_target_pairs={{0,24},{1,25},{2,26},{3,27},{4,28},{5,29},{6,30},{7,31},{8,16},{9,... | collective-permute-start | bytes 208904 | tf_op jit(solution)/shard_map/ppermute | solution.py:368
  105.0 50.9 %collective-permute-start.7 = (f32[136,128]{1,0:T(8,128)S(1)}, f32[136,128]{1,0:T(8,128)S(1)}, u32[]{:S(2)}, u32[]{:S(2)}) collective-permute-start(f32[136,128]{1,0:T(8,128)S(1)} %copy-done.13), channel_id=1, source_target_pairs={{0,16},{1,17},{2,18},{3,19},{4,20},{5,21},{6,22},{7,23},{8,24},{9,... | collective-permute-start | bytes 208904 | tf_op jit(solution)/shard_map/ppermute | solution.py:368
  105.0 50.9 %collective-permute-start.6 = (f32[136,128]{1,0:T(8,128)S(1)}, f32[136,128]{1,0:T(8,128)S(1)}, u32[]{:S(2)}, u32[]{:S(2)}) collective-permute-start(f32[136,128]{1,0:T(8,128)S(1)} %copy-done.13), channel_id=1, source_target_pairs={{0,8},{1,9},{2,10},{3,11},{4,12},{5,13},{6,14},{7,15},{8,0},{9,1},... | collective-permute-start | bytes 208904 | tf_op jit(solution)/shard_map/ppermute | solution.py:368
  141.7 14.2 %copy-start.16 = (f32[136,128]{1,0:T(8,128)}, f32[136,128]{1,0:T(8,128)S(1)}, u32[]{:S(2)}) copy-start(f32[136,128]{1,0:T(8,128)S(1)} %collective-permute-done.8.refs_3_) | copy-start | bytes 208900
  155.9 0.6 copy-start.17
  156.5 0.6 copy-start.19
  158.9 13.1 %copy-start.9 = (f32[544,128]{1,0:T(8,128)S(1)}, f32[544,128]{1,0:T(8,128)}, u32[]{:S(2)}) copy-start(f32[544,128]{1,0:T(8,128)} %shard_map.138.refs_0_) | copy-start | bytes 835588
  158.9 19.9 %collective-permute-start.11 = (f32[544,128]{1,0:T(8,128)}, f32[544,128]{1,0:T(8,128)}, u32[]{:S(2)}, u32[]{:S(2)}) collective-permute-start(f32[544,128]{1,0:T(8,128)} %shard_map.138.refs_0_), channel_id=1, source_target_pairs={{0,6},{1,7},{2,4},{3,5},{4,2},{5,3},{6,0},{7,1},{8,14},{9,15},{10,... | collective-permute-start | bytes 835592 | tf_op jit(solution)/shard_map/ppermute | solution.py:368
  161.3 18.1 %collective-permute-start.10 = (f32[544,128]{1,0:T(8,128)}, f32[544,128]{1,0:T(8,128)}, u32[]{:S(2)}, u32[]{:S(2)}) collective-permute-start(f32[544,128]{1,0:T(8,128)} %shard_map.138.refs_0_), channel_id=1, source_target_pairs={{0,4},{1,5},{2,6},{3,7},{4,0},{5,1},{6,2},{7,3},{8,12},{9,13},{10,... | collective-permute-start | bytes 835592 | tf_op jit(solution)/shard_map/ppermute | solution.py:368
  163.0 84.1 %collective-permute-start.3 = (f32[2048,128]{1,0:T(8,128)}, f32[2048,128]{1,0:T(8,128)}, u32[]{:S(2)}, u32[]{:S(2)}) collective-permute-start(f32[2048,128]{1,0:T(8,128)} %broadcast_select_fusion), channel_id=1, source_target_pairs={{0,2},{1,3},{2,0},{3,1},{4,6},{5,7},{6,4},{7,5},{8,10},{9,11},{10,... | collective-permute-start | bytes 3145736 | tf_op jit(solution)/shard_map/ppermute | solution.py:352
  163.5 6.2 %collective-permute-start.14 = (f32[136,128]{1,0:T(8,128)S(1)}, f32[136,128]{1,0:T(8,128)S(1)}, u32[]{:S(2)}, u32[]{:S(2)}) collective-permute-start(f32[136,128]{1,0:T(8,128)S(1)} %copy-done.4), channel_id=1, source_target_pairs={{0,24},{1,25},{2,26},{3,27},{4,28},{5,29},{6,30},{7,31},{8,16},{9,... | collective-permute-start | bytes 208904 | tf_op jit(solution)/shard_map/ppermute | solution.py:368
  166.6 5.4 %collective-permute-start.13 = (f32[136,128]{1,0:T(8,128)S(1)}, f32[136,128]{1,0:T(8,128)S(1)}, u32[]{:S(2)}, u32[]{:S(2)}) collective-permute-start(f32[136,128]{1,0:T(8,128)S(1)} %copy-done.4), channel_id=1, source_target_pairs={{0,16},{1,17},{2,18},{3,19},{4,20},{5,21},{6,22},{7,23},{8,24},{9,... | collective-permute-start | bytes 208904 | tf_op jit(solution)/shard_map/ppermute | solution.py:368
  169.7 4.3 %copy-start.14 = (f32[136,128]{1,0:T(8,128)}, f32[136,128]{1,0:T(8,128)S(1)}, u32[]{:S(2)}) copy-start(f32[136,128]{1,0:T(8,128)S(1)} %collective-permute-done.14.refs_3_) | copy-start | bytes 208900
  169.7 4.3 %collective-permute-start.12 = (f32[136,128]{1,0:T(8,128)S(1)}, f32[136,128]{1,0:T(8,128)S(1)}, u32[]{:S(2)}, u32[]{:S(2)}) collective-permute-start(f32[136,128]{1,0:T(8,128)S(1)} %copy-done.4), channel_id=1, source_target_pairs={{0,8},{1,9},{2,10},{3,11},{4,12},{5,13},{6,14},{7,15},{8,0},{9,1},... | collective-permute-start | bytes 208904 | tf_op jit(solution)/shard_map/ppermute | solution.py:368
  172.0 2.0 copy-start.15
  172.0 26.0 %collective-permute-start.9 = (f32[544,128]{1,0:T(8,128)S(1)}, f32[544,128]{1,0:T(8,128)S(1)}, u32[]{:S(2)}, u32[]{:S(2)}) collective-permute-start(f32[544,128]{1,0:T(8,128)S(1)} %copy-done.9), channel_id=1, source_target_pairs={{0,2},{1,3},{2,0},{3,1},{4,6},{5,7},{6,4},{7,5},{8,10},{9,11},{10,... | collective-permute-start | bytes 835592 | tf_op jit(solution)/shard_map/ppermute | solution.py:368
  174.0 0.6 copy-start.18
  176.3 47.6 %copy-start.20 = (f32[2048]{0:T(1024)S(1)}, f32[2048]{0:T(1024)}, u32[]{:S(2)}) copy-start(f32[2048]{0:T(1024)} %param.12) | copy-start | bytes 24580
  176.3 27.6 %collective-permute-start.17 = (f32[544,128]{1,0:T(8,128)}, f32[544,128]{1,0:T(8,128)S(1)}, u32[]{:S(2)}, u32[]{:S(2)}) collective-permute-start(f32[544,128]{1,0:T(8,128)} %shard_map.139.refs_4_), channel_id=1, source_target_pairs={{0,6},{1,7},{2,4},{3,5},{4,2},{5,3},{6,0},{7,1},{8,14},{9,15},{10,... | collective-permute-start | bytes 835592 | tf_op jit(solution)/shard_map/ppermute | solution.py:368
  178.8 25.2 %collective-permute-start.16 = (f32[544,128]{1,0:T(8,128)}, f32[544,128]{1,0:T(8,128)S(1)}, u32[]{:S(2)}, u32[]{:S(2)}) collective-permute-start(f32[544,128]{1,0:T(8,128)} %shard_map.139.refs_4_), channel_id=1, source_target_pairs={{0,4},{1,5},{2,6},{3,7},{4,0},{5,1},{6,2},{7,3},{8,12},{9,13},{10,... | collective-permute-start | bytes 835592 | tf_op jit(solution)/shard_map/ppermute | solution.py:368
  179.4 29.2 %collective-permute-start.15 = (f32[544,128]{1,0:T(8,128)}, f32[544,128]{1,0:T(8,128)}, u32[]{:S(2)}, u32[]{:S(2)}) collective-permute-start(f32[544,128]{1,0:T(8,128)} %shard_map.139.refs_4_), channel_id=1, source_target_pairs={{0,2},{1,3},{2,0},{3,1},{4,6},{5,7},{6,4},{7,5},{8,10},{9,11},{10,... | collective-permute-start | bytes 835592 | tf_op jit(solution)/shard_map/ppermute | solution.py:368
  197.9 10.6 %copy-start.10 = (f32[544,128]{1,0:T(8,128)}, f32[544,128]{1,0:T(8,128)S(1)}, u32[]{:S(2)}) copy-start(f32[544,128]{1,0:T(8,128)S(1)} %collective-permute-done.9.refs_1_) | copy-start | bytes 835588
  204.0 4.6 %copy-start.11 = (f32[544,128]{1,0:T(8,128)}, f32[544,128]{1,0:T(8,128)S(1)}, u32[]{:S(2)}) copy-start(f32[544,128]{1,0:T(8,128)S(1)} %collective-permute-done.17.refs_7_) | copy-start | bytes 835588
  204.0 4.6 %copy-start.12 = (f32[544,128]{1,0:T(8,128)}, f32[544,128]{1,0:T(8,128)S(1)}, u32[]{:S(2)}) copy-start(f32[544,128]{1,0:T(8,128)S(1)} %collective-permute-done.16.refs_6_) | copy-start | bytes 835588
  224.0 24.6 %collective-permute-start.18 = (f32[272,1024]{1,0:T(8,128)}, f32[272,1024]{1,0:T(8,128)}, u32[]{:S(2)}, u32[]{:S(2)}) collective-permute-start(f32[272,1024]{1,0:T(8,128)} %top.1), channel_id=1, source_target_pairs={{0,1},{1,0},{2,3},{3,2},{4,5},{5,4},{6,7},{7,6},{8,9},{9,8},{10,11... | collective-permute-start | bytes 3342344 | tf_op jit(solution)/shard_map/ppermute | solution.py:368
  224.0 3.1 %collective-permute-start.4 = (f32[16,128]{1,0:T(8,128)S(1)}, f32[16,128]{1,0:T(8,128)S(1)}, u32[]{:S(2)}, u32[]{:S(2)}) collective-permute-start(f32[16,128]{1,0:T(8,128)S(1)} %bitcast.32), channel_id=1, source_target_pairs={{0,1},{1,0},{2,3},{3,2},{4,5},{5,4},{6,7},{7,6},{8,9},{9,8},{10,11... | collective-permute-start | bytes 24584 | tf_op jit(solution)/shard_map/ppermute | solution.py:352
  227.1 20.0 %collective-permute-start.5 = (f32[16,128]{1,0:T(8,128)S(1)}, f32[16,128]{1,0:T(8,128)S(1)}, u32[]{:S(2)}, u32[]{:S(2)}) collective-permute-start(f32[16,128]{1,0:T(8,128)S(1)} %broadcast_select_fusion.4), channel_id=1, source_target_pairs={{0,2},{1,3},{2,0},{3,1},{4,6},{5,7},{6,4},{7,5},{8,10},{9,11},{10,... | collective-permute-start | bytes 24584 | tf_op jit(solution)/shard_map/ppermute | solution.py:352
  247.1 1.6 copy-start.7
  250.1 1.7 copy-start.6
  251.8 3.4 %copy-start = (bf16[2048,2048]{1,0:T(8,128)(2,1)S(1)}, bf16[2048,2048]{1,0:T(8,128)(2,1)}, u32[]{:S(2)}) copy-start(bf16[2048,2048]{1,0:T(8,128)(2,1)} %count.1.counts) | copy-start | bytes 25165828
where the time goes:
time: 262 us; the launch traced here: 261 us
  waiting for transfers between devices  132 us (50%)
  Pallas kernels  75.2 us (29%)
  starting transfers between devices  35.7 us (14%)
  local copies, waits for them, and re-layouts  10.7 us (4%)
  other arithmetic  5.44 us (2%)
    ppermute x13, waiting for transfers between devices, swap(): return lax.ppermute(value, AXES, [(d, d ^ offset) for d in range(devices)])  84.7 us
    all_to_all x3, waiting for transfers between devices, exchange(): return lax.all_to_all(x, AXES, split_axis=0, concat_axis=0, tiled=True)  44.7 us
    pallas_call x1, Pallas kernels, on_device(): pl.pallas_call(functools.partial(count_kernel, look_tiles, rows), out_sha...  18.5 us
    ppermute x13, starting transfers between devices, swap(): return lax.ppermute(value, AXES, [(d, d ^ offset) for d in range(devices)])  15.5 us
    pallas_call x1, Pallas kernels, on_device(): pl.pallas_call(functools.partial(top_kernel, len(near_dense)), out_shape=...  15.4 us
    all_to_all x3, starting transfers between devices, exchange(): return lax.all_to_all(x, AXES, split_axis=0, concat_axis=0, tiled=True)  14.1 us
    pallas_call x1, Pallas kernels, on_device(): pl.pallas_call(functools.partial(back_kernel, features, capacity), out_sh...  11 us
    pallas_call x1, Pallas kernels, on_device(): pl.pallas_call(functools.partial(pool_kernel, look_tiles, rows), out_shap...  9.44 us
  transfers between devices with their start and end apart: 22, of which 11 were waited for; matrix products, arithmetic and copies ran while one was open for 3% of the time, Pallas kernels for 19%

commit v1 on v0

--- a/solution.py
+++ b/solution.py
@@ -19,7 +19,7 @@
 BF16 = jnp.bfloat16
 VMEM = pl.BlockSpec(memory_space=pltpu.VMEM)
 SMEM = pl.BlockSpec(memory_space=pltpu.SMEM)
-ANY = pl.BlockSpec(memory_space=pl.ANY)
+HBM = pl.BlockSpec(memory_space=pltpu.HBM)
 
 
 def iota(shape, axis):
@@ -174,10 +174,6 @@
     return [(i, j) for i in range(features + 1) for j in range(i + 1, features + 1)]
 
 
-def tile_of(dense, vectors, samples, features, at):
-    return [dense[pl.ds(at, 8)]] + [vectors[pl.ds(f * samples + at, 8)] for f in range(features)]
-
-
 def scatter_rows(places, source, capacity, blocks, target):
     for s in range(places.shape[0]):
 
@@ -188,23 +184,30 @@
                 target[pl.ds(places[s, j], 1)] = part[j : j + 1]
 
 
-def gram_kernel(features, capacity, slots, source, got, dense, vectors, pairs, more):
+def gram_kernel(features, capacity, slots, source, got, dense, turned, pairs, vectors, partial):
     samples = dense.shape[0]
+    width = dense.shape[1]
     scatter_rows(slots, lambda s: source[s], capacity, got, vectors)
-    lane = iota((8, LANES), 1)
-
-    @pl.loop(0, samples // 8)
-    def _(t):
-        at = pl.multiple_of(t * 8, 8)
-        each = tile_of(dense, vectors, samples, features, at)
-        tiles = [jnp.zeros((8, LANES), F32) for _ in range(2)]
-        for p, (i, j) in enumerate(pairs_of(features)):
-            inner = jnp.sum(each[i] * each[j], axis=1, keepdims=True)
-            tiles[p // LANES] = jnp.where(lane == p % LANES, inner, tiles[p // LANES])
-        pairs[pl.ds(at, 8)] = tiles[0]
-        more[pl.ds(at, 8)] = tiles[1]
-
-    pairs[samples:] = more[...].T[: pairs.shape[0] - samples]
+    turned[:width] = dense[...].T
+    for f in range(features):
+        turned[(f + 1) * width : (f + 2) * width] = vectors[f * samples : (f + 1) * samples].T
+    p = 0
+    for i in range(features):
+        others = range(i + 1, features + 1)
+        sums = {}
+        for e in range(0, width, 8):
+            mine = turned[i * width + e : i * width + e + 8]
+            for j in others:
+                term = mine * turned[j * width + e : j * width + e + 8]
+                sums[j] = term if e == 0 else sums[j] + term
+        for j in others:
+            partial[p * 8 : p * 8 + 8] = sums[j]
+            p += 1
+    for q in range(0, p, 8):
+        total = partial[pl.ds(q * 8, 8, 8)]
+        for r in range(1, 8):
+            total = total + partial[pl.ds(q * 8 + r, 8, 8)]
+        pairs[q : q + 8] = total
 
 
 def halves_of(x):
@@ -232,8 +235,8 @@
 def inputs_of(dense, told):
     samples = dense.shape[0]
     dense_h, dense_l = halves_of(dense)
-    pairs_h, pairs_l = halves_of(told[:samples])
-    tail = told[samples:]
+    pairs_h, pairs_l = halves_of(told[:LANES].T)
+    tail = told[LANES:]
     tail_h = tail.astype(BF16).astype(F32)
     gap = jnp.zeros((LANES - 3 * tail.shape[0], samples), F32)
     rest = jnp.concatenate([tail_h, tail_h, tail - tail_h, gap], axis=0).T.astype(BF16)
@@ -250,27 +253,30 @@
     return hidden, d_logits, d_pre
 
 
-def back_kernel(features, capacity, slots, dense, vectors, pairs, labels, weight, left, out_weight, back, d_vectors, d_pairs, ready, sent):
+def back_kernel(features, capacity, slots, dense, turned, pairs, labels, weight, left, out_weight, back, d_vectors, d_turned, d_pairs, ready, sent):
     devices = slots.shape[0]
-    samples = dense.shape[0]
+    samples, width = dense.shape
     x = inputs_of(dense[...], pairs[...])
     _, _, d_pre = forward(x, column(labels[...])[:, :1], weight[...], out_weight[...])
     high, low = halves_of(d_pre)
-    d_pairs[...] = dot_t(jnp.concatenate([high, high, low], axis=1), left[...])
-
-    @pl.loop(0, samples // 8)
+    d_pairs[...] = dot_t(left[: d_pairs.shape[0]], jnp.concatenate([high, high, low], axis=1))
+    index = {pair: p for p, pair in enumerate(pairs_of(features))}
+
+    @pl.loop(0, width // 8)
     def _(t):
         at = pl.multiple_of(t * 8, 8)
-        each = tile_of(dense, vectors, samples, features, at)
-        slopes = d_pairs[pl.ds(at, 8)]
-        sums = [None] * (features + 1)
-        for p, (i, j) in enumerate(pairs_of(features)):
-            slope = jnp.broadcast_to(slopes[:, p : p + 1], (8, LANES))
-            if i > 0:
-                sums[i] = slope * each[j] if sums[i] is None else sums[i] + slope * each[j]
-            sums[j] = slope * each[i] if sums[j] is None else sums[j] + slope * each[i]
-        for f in range(features):
-            d_vectors[pl.ds(f * samples + at, 8)] = sums[f + 1]
+        each = [turned[pl.ds(f * width + at, 8)] for f in range(features + 1)]
+        for f in range(1, features + 1):
+            total = None
+            for j in range(features + 1):
+                if j != f:
+                    slope = d_pairs[pl.ds(index[min(f, j), max(f, j)], 8, 0)]
+                    term = slope * each[j]
+                    total = term if total is None else total + term
+            d_turned[pl.ds((f - 1) * width + at, 8)] = total
+
+    for f in range(features):
+        d_vectors[f * samples : (f + 1) * samples] = d_turned[f * width : (f + 1) * width].T
 
     def copy(s):
         part = pl.ds(pl.multiple_of(s * capacity, 8), capacity)
@@ -297,52 +303,41 @@
         refs[-1][n * size : (n + 1) * size] = ref[...]
 
 
-def top_kernel(parts, *refs):
-    dense_refs, pairs_refs = refs[:parts], refs[parts : 2 * parts]
-    weight, out_weight, grad, dense_all, pairs_all = refs[2 * parts :]
-    size = dense_refs[0].shape[0]
+def top_kernel(dense_told, pairs_told, weight, out_weight, before, grad):
     inter = grad.shape[0] - 8
     block = LANES + inter - 2 * LANES
-    for n in range(parts):
-        dense_all[n * size : (n + 1) * size] = dense_refs[n][...]
-        pairs_all[n * size : (n + 1) * size] = pairs_refs[n][...]
-    grad[...] = jnp.zeros_like(grad)
-
-    @pl.loop(0, parts)
-    def _(n):
-        xs, labels, columns = [], [], []
-        for m in range(size // block):
-            at = pl.ds(pl.multiple_of(n * size + m * block, 8), block)
-            rows, told = dense_all[at], pairs_all[at]
-            dense = rows[:LANES]
-            xs.append(inputs_of(dense, told))
-            labels.append(column(rows[LANES : LANES + 1])[:, :1])
-            columns.append(jnp.concatenate([dense.T, told[:LANES].T, told[LANES:], jnp.zeros((8, LANES), F32)], axis=0))
-        hidden, d_logits, d_pre = forward(
-            jnp.concatenate(xs, axis=0), jnp.concatenate(labels, axis=0), weight[...], out_weight[...]
-        )
-        x_high, x_low = halves_of(jnp.concatenate(columns, axis=1))
-        d_high, d_low = halves_of(d_pre)
-        grad[...] += dot(
-            jnp.concatenate([x_high, x_high, x_low], axis=1), jnp.concatenate([d_high, d_low, d_high], axis=0)
-        )
-        grad[inter:] += jnp.broadcast_to(jnp.sum(hidden * d_logits, axis=0, keepdims=True), (8, grad.shape[1]))
-
-
-def update_kernel(capacity, chunks, bags_s, came, counts, table, state, new_table, new_state, grads):
-    scatter_rows(bags_s, lambda s: s, capacity, came, grads)
-    parts = split(grads[...])
+    xs, labels, columns = [], [], []
+    for at in range(0, dense_told.shape[0], block):
+        dense, told = dense_told[at : at + LANES], pairs_told[at : at + block]
+        xs.append(inputs_of(dense, told))
+        labels.append(column(dense_told[at + LANES : at + LANES + 1])[:, :1])
+        columns.append(jnp.concatenate([dense.T, told, jnp.zeros((8, LANES), F32)], axis=0))
+    hidden, d_logits, d_pre = forward(
+        jnp.concatenate(xs, axis=0), jnp.concatenate(labels, axis=0), weight[...], out_weight[...]
+    )
+    x_high, x_low = halves_of(jnp.concatenate(columns, axis=1))
+    d_high, d_low = halves_of(d_pre)
+    total = dot(jnp.concatenate([x_high, x_high, x_low], axis=1), jnp.concatenate([d_high, d_low, d_high], axis=0))
+    grad[:inter] = before[:inter] + total[:inter]
+    last = jnp.sum(hidden * d_logits, axis=0, keepdims=True)
+    grad[inter:] = before[inter:] + jnp.broadcast_to(last, (8, grad.shape[1]))
+
+
+def update_kernel(capacity, bags_s, came, counts, table, state, new_table, new_state, grads, parts):
+    @pl.when(pl.program_id(0) == 0)
+    def _():
+        scatter_rows(bags_s, lambda s: s, capacity, came, grads)
+        parts[...] = split(grads[...])
+
+    row_grad = fold(dot(counts[...], parts[...]))
     width = grads.shape[1]
-    size = counts.shape[0] // chunks
-    for n in range(chunks):
-        row_grad = fold(dot(counts[n * size : (n + 1) * size], parts))
-        for j in range(size // LANES):
-            tile = n * (size // LANES) + j
-            at = slice(tile * LANES, (tile + 1) * LANES)
-            grad = row_grad[j * LANES : (j + 1) * LANES]
-            moved = column(state[tile : tile + 1]) + jnp.sum(grad * grad, axis=1, keepdims=True) / width
-            new_table[at] = table[at] - learn_rate * grad / (jnp.sqrt(moved) + epsilon)
-            new_state[tile : tile + 1] = moved.T[:1]
+    first = pl.program_id(0) * (counts.shape[0] // LANES)
+    for j in range(counts.shape[0] // LANES):
+        at = slice(j * LANES, (j + 1) * LANES)
+        grad = row_grad[at]
+        moved = column(state[pl.ds(first + j, 1)]) + jnp.sum(grad * grad, axis=1, keepdims=True) / width
+        new_table[at] = table[at] - learn_rate * grad / (jnp.sqrt(moved) + epsilon)
+        new_state[pl.ds(first + j, 1)] = moved.T[:1]
 
 
 def trade(values, pair_value):
@@ -376,15 +371,16 @@
         out_shape=jax.ShapeDtypeStruct((4 * value.shape[0], value.shape[1]), value.dtype),
         in_specs=[VMEM] * 4,
         out_specs=VMEM,
+        compiler_params=pltpu.CompilerParams(vmem_limit_bytes=4 << 20),
     )(*far)
     return [value] + [swap(value, k << bits - 4) for k in range(1, 4)]
 
 
-def sum_rest(value):
+def sum_rest(values):
     bits = (lax.axis_size("gx") * lax.axis_size("gy")).bit_length() - 1
     for bit in range(bits - 4):
-        value = value + swap(value, 1 << bit)
-    return value
+        values = jax.tree.map(lambda x: x + swap(x, 1 << bit), values)
+    return values
 
 
 def on_device(
@@ -455,6 +451,7 @@
         in_specs=[SMEM, VMEM],
         out_specs=pl.BlockSpec((table_rows, TILE), lambda i: (0, i)),
         scratch_shapes=[pltpu.VMEM((table_rows, TILE), F32)],
+        compiler_params=pltpu.CompilerParams(vmem_limit_bytes=24 << 20),
         name="count",
     )(meta, meta)
 
@@ -463,16 +460,17 @@
         out_shape=(shape((7 * LANES, hidden), BF16), shape((2 * LANES, 3 * hidden), BF16)),
         in_specs=[VMEM],
         out_specs=(VMEM, VMEM),
+        compiler_params=pltpu.CompilerParams(vmem_limit_bytes=24 << 20),
         name="weights",
     )(top_weight)
     out_row = out_weight.reshape(1, hidden)
-    block_scratch = [pltpu.VMEM((devices * capacity, width), F32), pltpu.SemaphoreType.DMA((devices,))]
-    vectors, pairs = pl.pallas_call(
+    pair_count = inter - width
+    turned, pairs = pl.pallas_call(
         functools.partial(gram_kernel, features, capacity),
-        out_shape=(shape((bags, width), F32), shape((samples + tail, LANES), F32)),
+        out_shape=(shape((bags + samples, width), F32), shape((pair_count, samples), F32)),
         in_specs=[SMEM, SMEM, VMEM, VMEM],
         out_specs=(VMEM, VMEM),
-        scratch_shapes=[pltpu.VMEM((samples, LANES), F32)],
+        scratch_shapes=[pltpu.VMEM((bags, width), F32), pltpu.VMEM((8 * pair_count, samples), F32)],
         compiler_params=pltpu.CompilerParams(vmem_limit_bytes=16 << 20),
         name="gram",
     )(got_slots, source, in_vmem(got), dense_vectors)
@@ -483,36 +481,55 @@
         functools.partial(back_kernel, features, capacity),
         out_shape=shape((devices * capacity, width), F32),
         in_specs=[SMEM] + [VMEM] * 7,
-        out_specs=ANY,
-        scratch_shapes=[pltpu.VMEM((bags, width), F32), pltpu.VMEM((samples, 2 * LANES), F32)] + block_scratch,
+        out_specs=HBM,
+        scratch_shapes=[
+            pltpu.VMEM((bags, width), F32),
+            pltpu.VMEM((bags, samples), F32),
+            pltpu.VMEM((pair_count + 8, samples), F32),
+            pltpu.VMEM((devices * capacity, width), F32),
+            pltpu.SemaphoreType.DMA((devices,)),
+        ],
+        compiler_params=pltpu.CompilerParams(vmem_limit_bytes=58 << 20),
         name="back",
-    )(got_slots, dense_vectors, vectors, pairs, labels.reshape(1, samples), right, left, out_row)
+    )(
+        got_slots,
+        dense_vectors,
+        in_vmem(turned),
+        in_vmem(pairs),
+        labels.reshape(1, samples),
+        in_vmem(right),
+        in_vmem(left),
+        out_row,
+    )
     came = exchange(back.reshape(devices, capacity, width))
     came = came.reshape(devices * capacity, width)
 
-    gathered = len(near_dense) * near_dense[0].shape[0]
-    local = pl.pallas_call(
-        functools.partial(top_kernel, len(near_dense)),
-        out_shape=shape((inter + 8, hidden), F32),
-        in_specs=[VMEM] * (2 * len(near_dense) + 2),
-        out_specs=VMEM,
-        scratch_shapes=[pltpu.VMEM((gathered, LANES), F32)] * 2,
-        name="top",
-    )(*near_dense, *near_pairs, right, out_row)
-    summed = sum_rest(local)
+    local = jnp.zeros((inter + 8, hidden), F32)
+    for dense_part, pairs_part in zip(near_dense, near_pairs):
+        local = pl.pallas_call(
+            top_kernel,
+            out_shape=shape((inter + 8, hidden), F32),
+            in_specs=[VMEM] * 5,
+            out_specs=VMEM,
+            compiler_params=pltpu.CompilerParams(vmem_limit_bytes=24 << 20),
+            name="top",
+        )(dense_part, pairs_part, right, out_row, local)
+    top_grad, out_grad = sum_rest((local[:inter], local[inter]))
 
     chunks = 4
+    piece = pl.BlockSpec((table_rows // chunks, width), lambda i: (i, 0))
     update = pl.pallas_call(
-        functools.partial(update_kernel, capacity, chunks),
+        functools.partial(update_kernel, capacity),
         out_shape=(shape((table_rows, width), F32), shape((table_rows // LANES, LANES), F32)),
-        in_specs=[SMEM] + [VMEM] * 4,
-        out_specs=(VMEM, VMEM),
-        scratch_shapes=[pltpu.VMEM((bags, width), F32)],
-        compiler_params=pltpu.CompilerParams(vmem_limit_bytes=24 << 20),
+        grid=(chunks,),
+        in_specs=[SMEM, VMEM, pl.BlockSpec((table_rows // chunks, bags), lambda i: (i, 0)), piece, VMEM],
+        out_specs=(piece, pl.BlockSpec((table_rows // LANES, LANES), lambda i: (0, 0))),
+        scratch_shapes=[pltpu.VMEM((bags, width), F32), pltpu.VMEM((bags, 2 * width), BF16)],
+        compiler_params=pltpu.CompilerParams(vmem_limit_bytes=56 << 20),
         name="update",
     )
-    new_table, new_state = update(places, in_vmem(came), in_vmem(counts), in_vmem(held_table), held_state)
-    return new_table, new_state.reshape(-1), summed[:inter], summed[inter]
+    new_table, new_state = update(places, in_vmem(came), counts, held_table, held_state)
+    return new_table, new_state.reshape(-1), top_grad, out_grad
 
 
 def solution(mesh):

time: 262 us -> 242 us (0.924)
  waiting for transfers between devices: 132 us -> 110 us
  starting transfers between devices: 35.7 us -> 53.2 us
  Pallas kernels: 75.2 us -> 61 us
    ppermute x13 -> x14, waiting for transfers between devices: 84.7 us -> 61.7 us  [swap(): return lax.ppermute(value, AXES, [(d, d ^ offset) for d in range(devices)])]
    ppermute x13 -> x14, starting transfers between devices: 15.5 us -> 33.4 us  [swap(): return lax.ppermute(value, AXES, [(d, d ^ offset) for d in range(devices)])]
    pallas_call x1, Pallas kernels: 11 us -> 6.11 us  [on_device(): pl.pallas_call(functools.partial(back_kernel, features, capacity), out_sh...]
    pallas_call x2, Pallas kernels: 3.42 us -> 0.04 us  [gather_near(): pl.pallas_call(pack_kernel, out_shape=jax.ShapeDtypeStruct((4 * value.sha...]
    pallas_call x1, Pallas kernels: 3.3 us -> 0.27 us  [on_device(): pl.pallas_call(weight_kernel, out_shape=(shape((7 * LANES, hidden), BF16)...]
    unnamed x42 -> x28, local copies, waits for them, and re-layouts: 7.04 us -> 8.58 us
    pallas_call x2 -> x5, Pallas kernels: 21.2 us -> 20.9 us  [the longest x4 12.6 us: on_device(): pl.pallas_call(top_kernel, out_shape=shape((inter + 8, hidden), F32), in_...]
  transfers between devices with their start and end apart: 22 -> 23, of which waited for: 11 -> 12; matrix products, arithmetic and copies ran while one was open for 3% -> 3% of each run, Pallas kernels for 19% -> 17%
where the time goes in v1:
time: 242 us; the launch traced here: 241 us
  waiting for transfers between devices  110 us (45%)
  Pallas kernels  61 us (25%)
  starting transfers between devices  53.2 us (22%)
  local copies, waits for them, and re-layouts  10.8 us (4%)
  other arithmetic  4.95 us (2%)
    ppermute x14, waiting for transfers between devices, swap(): return lax.ppermute(value, AXES, [(d, d ^ offset) for d in range(devices)])  61.7 us
    all_to_all x3, waiting for transfers between devices, exchange(): return lax.all_to_all(x, AXES, split_axis=0, concat_axis=0, tiled=True)  45.4 us
    ppermute x14, starting transfers between devices, swap(): return lax.ppermute(value, AXES, [(d, d ^ offset) for d in range(devices)])  33.4 us
    pallas_call x1, Pallas kernels, on_device(): pl.pallas_call(functools.partial(count_kernel, look_tiles, rows), out_sha...  18.4 us
    all_to_all x3, starting transfers between devices, exchange(): return lax.all_to_all(x, AXES, split_axis=0, concat_axis=0, tiled=True)  14.1 us
    pallas_call x4, Pallas kernels, on_device(): pl.pallas_call(top_kernel, out_shape=shape((inter + 8, hidden), F32), in_...  12.6 us
    pallas_call x1, Pallas kernels, on_device(): pl.pallas_call(functools.partial(pool_kernel, look_tiles, rows), out_shap...  9.45 us
    unnamed x28, local copies, waits for them, and re-layouts  8.58 us
  transfers between devices with their start and end apart: 23, of which 12 were waited for; matrix products, arithmetic and copies ran while one was open for 3% of the time, Pallas kernels for 17%

profile of v1, /device:TPU:0, one launch (start us, length us, event | category | flops | bytes accessed | tf_op | source)
XLA Modules:
  0.0 241.3 jit_solution(12886033279923779646)
XLA Ops:
  0.6 2.6 %prep.1 = (s32[104,128]{1,0:T(8,128)}, s32[32,128]{1,0:T(8,128)}, s32[32,128]{1,0:T(8,128)}, f32[136,128]{1,0:T(8,128)}) custom-call(s32[48,128]{1,0:T(8,128)} %bitcast.38, s32[16,128]{1,0:T(8,128)} %bitcast.42, s32[16,128]{1,0:T(8,128)} %bitcast.43, s32[16,128]{1,0:T(8,128)} %bitcast.44, f32[128,128]{1,0:T(8,128)} %dense.3, f32[1,128]{1,0:T(1,128)} %bitcast.45), custom_call_target="tpu_custom_call" | custom-call | tf_op jit(solution)/shard_map/prep/pallas_call | solution.py:402
  3.3 0.5 collective-permute-start
  4.9 0.8 broadcast_select_fusion.2
  5.7 2.8 %collective-permute-start.1 = (s32[104,128]{1,0:T(8,128)S(1)}, s32[104,128]{1,0:T(8,128)S(1)}, u32[]{:S(2)}, u32[]{:S(2)}) collective-permute-start(s32[104,128]{1,0:T(8,128)S(1)} %broadcast_select_fusion.2), channel_id=1, source_target_pairs={{0,2},{1,3},{2,0},{3,1},{4,6},{5,7},{6,4},{7,5},{8,10},{9,11},{10,... | collective-permute-start | bytes 159752 | tf_op jit(solution)/shard_map/ppermute | solution.py:347
  8.5 1.3 stack.7.clone
  9.8 4.2 %all-to-all-start = ((s32[32,2,128]{2,1,0:T(2,128)}), s32[32,2,128]{2,1,0:T(2,128)S(1)}, u32[]{:S(2)}, u32[]{:S(2)}) async-start(s32[32,2,128]{2,1,0:T(2,128)} %stack.7.clone), calls=%async_computation | async-start | bytes 65536 | tf_op jit(solution)/shard_map/all_to_all | solution.py:354
  14.0 0.6 broadcast_select_fusion.3.meta_s.meta_v
  14.7 9.5 %pool.1 = f32[4096,128]{1,0:T(8,128)} custom-call(s32[104,128]{1,0:T(8,128)} %broadcast_select_fusion.3.meta_s.meta_v, s32[104,128]{1,0:T(8,128)} %broadcast_select_fusion.3.meta_s.meta_v, f32[2048,128]{1,0:T(8,128)} %table.1), custom_call_target="tpu_custom_call" | custom-call | tf_op jit(solution)/shard_map/pool/pallas_call | solution.py:427
  24.1 5.8 %all-to-all-start.1 = ((f32[32,128,128]{2,1,0:T(8,128)}), f32[32,128,128]{2,1,0:T(8,128)S(1)}, u32[]{:S(2)}, u32[]{:S(2)}) async-start(f32[32,128,128]{2,1,0:T(8,128)} %bitcast.35), calls=%async_computation.1 | async-start | bytes 4194304 | tf_op jit(solution)/shard_map/all_to_all | solution.py:354
  30.3 1.2 copy-done
  31.5 1.2 copy-done.4
  32.7 0.7 slice_reduce_fusion
  33.3 45.4 %all-to-all-done.1 = f32[32,128,128]{2,1,0:T(8,128)S(1)} async-done(((f32[32,128,128]{2,1,0:T(8,128)}), f32[32,128,128]{2,1,0:T(8,128)S(1)}, u32[]{:S(2)}, u32[]{:S(2)}) %all-to-all-start.1) | async-done | bytes 2097184 | tf_op jit(solution)/shard_map/all_to_all | solution.py:354
  78.7 1.0 copy-done.7
  79.7 3.1 %gram.1 = (f32[2176,128]{1,0:T(8,128)S(1)}, f32[136,128]{1,0:T(8,128)S(1)}) custom-call(s32[32,128]{1,0:T(8,128)S(1)} %bitcast.28, s32[32]{0:T(128)S(1)} %iota_xor_fusion.source, f32[4096,128]{1,0:T(8,128)S(1)} %bitcast.27, f32[128,128]{1,0:T(8,128)S(1)} %copy-done.7), custom_call_target="tpu_custom_call" | custom-call | tf_op jit(solution)/shard_map/gram/pallas_call | solution.py:468
  82.8 1.4 copy-done.5
  84.2 6.1 %back.1 = f32[4096,128]{1,0:T(8,128)} custom-call(s32[32,128]{1,0:T(8,128)} %bitcast.29, f32[128,128]{1,0:T(8,128)} %dense.3, f32[2176,128]{1,0:T(8,128)S(1)} %get-tuple-element.21.turned, f32[136,128]{1,0:T(8,128)S(1)} %get-tuple-element.22.pairs.refs_0_, f32[1,128]{1,0:T(1,128)} %bitcast.46, bf16[896,1024]{1,0:T(8,128)(2,1)S(1)} %copy-done.1, ...), custom_call_target="tpu_custom_call" | custom-call | tf_op jit(solution)/shard_map/back/pallas_call | solution.py:480
  90.4 4.1 %all-to-all-start.2 = ((f32[32,128,128]{2,1,0:T(8,128)}), f32[32,128,128]{2,1,0:T(8,128)S(1)}, u32[]{:S(2)}, u32[]{:S(2)}) async-start(f32[32,128,128]{2,1,0:T(8,128)} %bitcast.36), calls=%async_computation.2 | async-start | bytes 4194304 | tf_op jit(solution)/shard_map/all_to_all | solution.py:354
  94.8 3.5 %collective-permute-start.8 = (f32[136,128]{1,0:T(8,128)S(1)}, f32[136,128]{1,0:T(8,128)S(1)}, u32[]{:S(2)}, u32[]{:S(2)}) collective-permute-start(f32[136,128]{1,0:T(8,128)S(1)} %copy-done.11), channel_id=1, source_target_pairs={{0,24},{1,25},{2,26},{3,27},{4,28},{5,29},{6,30},{7,31},{8,16},{9,... | collective-permute-start | bytes 208904 | tf_op jit(solution)/shard_map/ppermute | solution.py:363
  98.3 0.9 collective-permute-start.6
  99.2 3.5 %collective-permute-start.12 = (f32[136,128]{1,0:T(8,128)S(1)}, f32[136,128]{1,0:T(8,128)S(1)}, u32[]{:S(2)}, u32[]{:S(2)}) collective-permute-start(f32[136,128]{1,0:T(8,128)S(1)} %get-tuple-element.22.pairs.refs_0_), channel_id=1, source_target_pairs={{0,24},{1,25},{2,26},{3,27},{4,28},{5,29},{6,30},{7,31},{8,16},{9,... | collective-permute-start | bytes 208904 | tf_op jit(solution)/shard_map/ppermute | solution.py:363
  102.7 32.3 %collective-permute-done.8.refs_3_ = f32[136,128]{1,0:T(8,128)S(1)} collective-permute-done((f32[136,128]{1,0:T(8,128)S(1)}, f32[136,128]{1,0:T(8,128)S(1)}, u32[]{:S(2)}, u32[]{:S(2)}) %collective-permute-start.8) | collective-permute-done | bytes 69664 | tf_op jit(solution)/shard_map/ppermute | solution.py:363
  135.0 15.2 %collective-permute-start.11 = (f32[136,128]{1,0:T(8,128)S(1)}, f32[136,128]{1,0:T(8,128)S(1)}, u32[]{:S(2)}, u32[]{:S(2)}) collective-permute-start(f32[136,128]{1,0:T(8,128)S(1)} %get-tuple-element.22.pairs.refs_0_), channel_id=1, source_target_pairs={{0,16},{1,17},{2,18},{3,19},{4,20},{5,21},{6,22},{7,23},{8,24},{9,... | collective-permute-start | bytes 208904 | tf_op jit(solution)/shard_map/ppermute | solution.py:363
  150.2 1.0 collective-permute-done.7.refs_2_
  151.3 1.6 collective-permute-start.16
  152.9 2.3 collective-permute-done.11.refs_2_
  155.7 1.6 collective-permute-start.17
  157.4 0.5 collective-permute-start.3
  157.9 1.4 collective-permute-start.14
  159.4 0.6 collective-permute-start.15
  160.3 2.4 %collective-permute-start.9 = (f32[544,128]{1,0:T(8,128)S(1)}, f32[544,128]{1,0:T(8,128)S(1)}, u32[]{:S(2)}, u32[]{:S(2)}) collective-permute-start(f32[544,128]{1,0:T(8,128)S(1)} %shard_map.138.dense_told), channel_id=1, source_target_pairs={{0,6},{1,7},{2,4},{3,5},{4,2},{5,3},{6,0},{7,1},{8,14},{9,15},{10,... | collective-permute-start | bytes 835592 | tf_op jit(solution)/shard_map/ppermute | solution.py:363
  162.8 3.5 %collective-permute-done.17.pairs_told = f32[544,128]{1,0:T(8,128)S(1)} collective-permute-done((f32[544,128]{1,0:T(8,128)S(1)}, f32[544,128]{1,0:T(8,128)S(1)}, u32[]{:S(2)}, u32[]{:S(2)}) %collective-permute-start.17) | collective-permute-done | bytes 278560 | tf_op jit(solution)/shard_map/ppermute | solution.py:363
  166.3 2.4 %collective-permute-start.13 = (f32[544,128]{1,0:T(8,128)S(1)}, f32[544,128]{1,0:T(8,128)S(1)}, u32[]{:S(2)}, u32[]{:S(2)}) collective-permute-start(f32[544,128]{1,0:T(8,128)S(1)} %shard_map.139.pairs_told), channel_id=1, source_target_pairs={{0,6},{1,7},{2,4},{3,5},{4,2},{5,3},{6,0},{7,1},{8,14},{9,15},{10,... | collective-permute-start | bytes 835592 | tf_op jit(solution)/shard_map/ppermute | solution.py:363
  168.9 3.1 %top.4.before = f32[272,1024]{1,0:T(8,128)S(1)} custom-call(f32[544,128]{1,0:T(8,128)S(1)} %shard_map.138.dense_told, f32[544,128]{1,0:T(8,128)S(1)} %shard_map.139.pairs_told, bf16[896,1024]{1,0:T(8,128)(2,1)S(1)} %copy-done.2, f32[1,1024]{1,0:T(1,128)S(1)} %bitcast.31, f32[272,1024]{1,0:T(8,128)S(1)} %broadcast_in_dim.3.before), custom_call_target="tpu_custom_call" | custom-call | tf_op jit(solution)/shard_map/top/pallas_call | solution.py:509
  172.1 3.2 %top.5.before = f32[272,1024]{1,0:T(8,128)S(1)} custom-call(f32[544,128]{1,0:T(8,128)S(1)} %collective-permute-done.16.dense_told, f32[544,128]{1,0:T(8,128)S(1)} %collective-permute-done.17.pairs_told, bf16[896,1024]{1,0:T(8,128)(2,1)S(1)} %copy-done.2, f32[1,1024]{1,0:T(1,128)S(1)} %bitcast.32, f32[272,1024]{1,0:T(8,128)S(1)} %top.4.before), custom_call_target="tpu_custom_call" | custom-call | tf_op jit(solution)/shard_map/top/pallas_call | solution.py:509
  175.2 3.1 %top.6.before = f32[272,1024]{1,0:T(8,128)S(1)} custom-call(f32[544,128]{1,0:T(8,128)S(1)} %collective-permute-done.14.dense_told, f32[544,128]{1,0:T(8,128)S(1)} %collective-permute-done.15.pairs_told, bf16[896,1024]{1,0:T(8,128)(2,1)S(1)} %copy-done.2, f32[1,1024]{1,0:T(1,128)S(1)} %bitcast.33, f32[272,1024]{1,0:T(8,128)S(1)} %top.5.before), custom_call_target="tpu_custom_call" | custom-call | tf_op jit(solution)/shard_map/top/pallas_call | solution.py:509
  178.4 17.2 %collective-permute-done.9.dense_told = f32[544,128]{1,0:T(8,128)S(1)} collective-permute-done((f32[544,128]{1,0:T(8,128)S(1)}, f32[544,128]{1,0:T(8,128)S(1)}, u32[]{:S(2)}, u32[]{:S(2)}) %collective-permute-start.9) | collective-permute-done | bytes 278560 | tf_op jit(solution)/shard_map/ppermute | solution.py:363
  195.6 4.5 %collective-permute-done.13.pairs_told = f32[544,128]{1,0:T(8,128)S(1)} collective-permute-done((f32[544,128]{1,0:T(8,128)S(1)}, f32[544,128]{1,0:T(8,128)S(1)}, u32[]{:S(2)}, u32[]{:S(2)}) %collective-permute-start.13) | collective-permute-done | bytes 278560 | tf_op jit(solution)/shard_map/ppermute | solution.py:363
  200.1 3.2 %top.7 = f32[272,1024]{1,0:T(8,128)S(1)} custom-call(f32[544,128]{1,0:T(8,128)S(1)} %collective-permute-done.9.dense_told, f32[544,128]{1,0:T(8,128)S(1)} %collective-permute-done.13.pairs_told, bf16[896,1024]{1,0:T(8,128)(2,1)S(1)} %copy-done.2, f32[1,1024]{1,0:T(1,128)S(1)} %bitcast.34, f32[272,1024]{1,0:T(8,128)S(1)} %top.6.before), custom_call_target="tpu_custom_call" | custom-call | tf_op jit(solution)/shard_map/top/pallas_call | solution.py:509
  204.0 2.2 collective-permute-done.4
  206.2 1.6 collective-permute-start.5
  207.8 18.4 %count.1.counts = bf16[2048,2048]{1,0:T(8,128)(2,1)S(1)} custom-call(s32[104,128]{1,0:T(8,128)S(1)} %copy-done.8, s32[104,128]{1,0:T(8,128)S(1)} %copy-done.8), custom_call_target="tpu_custom_call" | custom-call | tf_op jit(solution)/shard_map/count/pallas_call | solution.py:447
  226.2 3.3 %copy-done.3 = bf16[2048,2048]{1,0:T(8,128)(2,1)} copy-done((bf16[2048,2048]{1,0:T(8,128)(2,1)}, bf16[2048,2048]{1,0:T(8,128)(2,1)S(1)}, u32[]{:S(2)}) %copy-start.3) | copy-done | bytes 8388632
  229.5 0.6 broadcast_select_fusion.5.state
  230.1 1.1 broadcast_select_fusion.1.table
  231.2 0.6 add.9
  231.8 1.1 slice_add_fusion
  233.0 8.3 %update.1 = (f32[2048,128]{1,0:T(8,128)}, f32[16,128]{1,0:T(8,128)}) custom-call(s32[32,128]{1,0:T(8,128)} %get-tuple-element.16.bags_s, f32[4096,128]{1,0:T(8,128)S(1)} %bitcast.26, bf16[2048,2048]{1,0:T(8,128)(2,1)} %copy-done.3, f32[2048,128]{1,0:T(8,128)} %broadcast_select_fusion.1.table, f32[16,128]{1,0:T(8,128)} %broadcast_select_fusion.5.state), custom_call_target="tpu_custom_call" | custom-call | tf_op jit(solution)/shard_map/update/pallas_call | solution.py:531
  (54 shorter events, 2.9 us)
Async XLA Ops:
  3.3 1.6 collective-permute-start
  5.7 8.3 %collective-permute-start.1 = (s32[104,128]{1,0:T(8,128)S(1)}, s32[104,128]{1,0:T(8,128)S(1)}, u32[]{:S(2)}, u32[]{:S(2)}) collective-permute-start(s32[104,128]{1,0:T(8,128)S(1)} %broadcast_select_fusion.2), channel_id=1, source_target_pairs={{0,2},{1,3},{2,0},{3,1},{4,6},{5,7},{6,4},{7,5},{8,10},{9,11},{10,... | collective-permute-start | bytes 159752 | tf_op jit(solution)/shard_map/ppermute | solution.py:347
  9.8 14.3 %all-to-all-start = ((s32[32,2,128]{2,1,0:T(2,128)}), s32[32,2,128]{2,1,0:T(2,128)S(1)}, u32[]{:S(2)}, u32[]{:S(2)}) async-start(s32[32,2,128]{2,1,0:T(2,128)} %stack.7.clone), calls=%async_computation | async-start | bytes 65536 | tf_op jit(solution)/shard_map/all_to_all | solution.py:354
  24.1 5.8 %copy-start.6 = (f32[264,1024]{1,0:T(8,128)S(1)}, f32[264,1024]{1,0:T(8,128)}, u32[]{:S(2)}) copy-start(f32[264,1024]{1,0:T(8,128)} %weight.1) | copy-start | bytes 3244036
  24.1 54.6 %all-to-all-start.1 = ((f32[32,128,128]{2,1,0:T(8,128)}), f32[32,128,128]{2,1,0:T(8,128)S(1)}, u32[]{:S(2)}, u32[]{:S(2)}) async-start(f32[32,128,128]{2,1,0:T(8,128)} %bitcast.35), calls=%async_computation.1 | async-start | bytes 4194304 | tf_op jit(solution)/shard_map/all_to_all | solution.py:354
  30.2 1.2 copy-start
  31.5 1.2 copy-start.4
  32.7 50.1 %copy-start.9 = (s32[32,1,128]{2,1,0:T(1,128)}, s32[32,1,128]{2,1,0:T(1,128)S(1)}, u32[]{:S(2)}) copy-start(s32[32,1,128]{2,1,0:T(1,128)S(1)} %slice.16) | copy-start | bytes 49156
  78.7 4.1 %copy-start.1 = (bf16[896,1024]{1,0:T(8,128)(2,1)S(1)}, bf16[896,1024]{1,0:T(8,128)(2,1)}, u32[]{:S(2)}) copy-start(bf16[896,1024]{1,0:T(8,128)(2,1)} %copy-done) | copy-start | bytes 5505028
  78.7 1.0 copy-start.7
  82.8 1.4 copy-start.5
  90.4 4.4 %copy-start.11 = (f32[136,128]{1,0:T(8,128)S(1)}, f32[136,128]{1,0:T(8,128)}, u32[]{:S(2)}) copy-start(f32[136,128]{1,0:T(8,128)} %get-tuple-element.27.refs_0_) | copy-start | bytes 208900
  90.4 142.6 %all-to-all-start.2 = ((f32[32,128,128]{2,1,0:T(8,128)}), f32[32,128,128]{2,1,0:T(8,128)S(1)}, u32[]{:S(2)}, u32[]{:S(2)}) async-start(f32[32,128,128]{2,1,0:T(8,128)} %bitcast.36), calls=%async_computation.2 | async-start | bytes 4194304 | tf_op jit(solution)/shard_map/all_to_all | solution.py:354
  94.5 62.8 %copy-start.12 = (f32[2048,128]{1,0:T(8,128)S(1)}, f32[2048,128]{1,0:T(8,128)}, u32[]{:S(2)}) copy-start(f32[2048,128]{1,0:T(8,128)} %table.1) | copy-start | bytes 3145732
  94.5 62.8 %collective-permute-start.2 = (f32[2048,128]{1,0:T(8,128)}, f32[2048,128]{1,0:T(8,128)S(1)}, u32[]{:S(2)}, u32[]{:S(2)}) collective-permute-start(f32[2048,128]{1,0:T(8,128)} %table.1), channel_id=1, source_target_pairs={{0,1},{1,0},{2,3},{3,2},{4,5},{5,4},{6,7},{7,6},{8,9},{9,8},{10,11... | collective-permute-start | bytes 3145736 | tf_op jit(solution)/shard_map/ppermute | solution.py:347
  94.8 40.2 %collective-permute-start.8 = (f32[136,128]{1,0:T(8,128)S(1)}, f32[136,128]{1,0:T(8,128)S(1)}, u32[]{:S(2)}, u32[]{:S(2)}) collective-permute-start(f32[136,128]{1,0:T(8,128)S(1)} %copy-done.11), channel_id=1, source_target_pairs={{0,24},{1,25},{2,26},{3,27},{4,28},{5,29},{6,30},{7,31},{8,16},{9,... | collective-permute-start | bytes 208904 | tf_op jit(solution)/shard_map/ppermute | solution.py:363
  98.3 52.9 %collective-permute-start.7 = (f32[136,128]{1,0:T(8,128)S(1)}, f32[136,128]{1,0:T(8,128)S(1)}, u32[]{:S(2)}, u32[]{:S(2)}) collective-permute-start(f32[136,128]{1,0:T(8,128)S(1)} %copy-done.11), channel_id=1, source_target_pairs={{0,16},{1,17},{2,18},{3,19},{4,20},{5,21},{6,22},{7,23},{8,24},{9,... | collective-permute-start | bytes 208904 | tf_op jit(solution)/shard_map/ppermute | solution.py:363
  98.3 52.9 %collective-permute-start.6 = (f32[136,128]{1,0:T(8,128)S(1)}, f32[136,128]{1,0:T(8,128)S(1)}, u32[]{:S(2)}, u32[]{:S(2)}) collective-permute-start(f32[136,128]{1,0:T(8,128)S(1)} %copy-done.11), channel_id=1, source_target_pairs={{0,8},{1,9},{2,10},{3,11},{4,12},{5,13},{6,14},{7,15},{8,0},{9,1},... | collective-permute-start | bytes 208904 | tf_op jit(solution)/shard_map/ppermute | solution.py:363
  99.2 53.7 %collective-permute-start.12 = (f32[136,128]{1,0:T(8,128)S(1)}, f32[136,128]{1,0:T(8,128)S(1)}, u32[]{:S(2)}, u32[]{:S(2)}) collective-permute-start(f32[136,128]{1,0:T(8,128)S(1)} %get-tuple-element.22.pairs.refs_0_), channel_id=1, source_target_pairs={{0,24},{1,25},{2,26},{3,27},{4,28},{5,29},{6,30},{7,31},{8,16},{9,... | collective-permute-start | bytes 208904 | tf_op jit(solution)/shard_map/ppermute | solution.py:363
  135.0 20.3 %collective-permute-start.11 = (f32[136,128]{1,0:T(8,128)S(1)}, f32[136,128]{1,0:T(8,128)S(1)}, u32[]{:S(2)}, u32[]{:S(2)}) collective-permute-start(f32[136,128]{1,0:T(8,128)S(1)} %get-tuple-element.22.pairs.refs_0_), channel_id=1, source_target_pairs={{0,16},{1,17},{2,18},{3,19},{4,20},{5,21},{6,22},{7,23},{8,24},{9,... | collective-permute-start | bytes 208904 | tf_op jit(solution)/shard_map/ppermute | solution.py:363
  151.2 4.4 %collective-permute-start.10 = (f32[136,128]{1,0:T(8,128)S(1)}, f32[136,128]{1,0:T(8,128)S(1)}, u32[]{:S(2)}, u32[]{:S(2)}) collective-permute-start(f32[136,128]{1,0:T(8,128)S(1)} %get-tuple-element.22.pairs.refs_0_), channel_id=1, source_target_pairs={{0,8},{1,9},{2,10},{3,11},{4,12},{5,13},{6,14},{7,15},{8,0},{9,1},... | collective-permute-start | bytes 208904 | tf_op jit(solution)/shard_map/ppermute | solution.py:363
  151.3 9.1 %collective-permute-start.16 = (f32[544,128]{1,0:T(8,128)S(1)}, f32[544,128]{1,0:T(8,128)S(1)}, u32[]{:S(2)}, u32[]{:S(2)}) collective-permute-start(f32[544,128]{1,0:T(8,128)S(1)} %shard_map.138.dense_told), channel_id=1, source_target_pairs={{0,2},{1,3},{2,0},{3,1},{4,6},{5,7},{6,4},{7,5},{8,10},{9,11},{10,... | collective-permute-start | bytes 835592 | tf_op jit(solution)/shard_map/ppermute | solution.py:363
  155.7 10.7 %collective-permute-start.17 = (f32[544,128]{1,0:T(8,128)S(1)}, f32[544,128]{1,0:T(8,128)S(1)}, u32[]{:S(2)}, u32[]{:S(2)}) collective-permute-start(f32[544,128]{1,0:T(8,128)S(1)} %shard_map.139.pairs_told), channel_id=1, source_target_pairs={{0,2},{1,3},{2,0},{3,1},{4,6},{5,7},{6,4},{7,5},{8,10},{9,11},{10,... | collective-permute-start | bytes 835592 | tf_op jit(solution)/shard_map/ppermute | solution.py:363
  157.3 11.6 %copy-start.2 = (bf16[896,1024]{1,0:T(8,128)(2,1)S(1)}, bf16[896,1024]{1,0:T(8,128)(2,1)}, u32[]{:S(2)}) copy-start(bf16[896,1024]{1,0:T(8,128)(2,1)} %copy-done) | copy-start | bytes 5505028
  157.4 11.5 %copy-start.10 = (f32[1024]{0:T(1024)S(1)}, f32[1024]{0:T(1024)}, u32[]{:S(2)}) copy-start(f32[1024]{0:T(1024)} %param.21) | copy-start | bytes 12292
  157.4 72.7 %collective-permute-start.3 = (f32[2048,128]{1,0:T(8,128)S(1)}, f32[2048,128]{1,0:T(8,128)S(1)}, u32[]{:S(2)}, u32[]{:S(2)}) collective-permute-start(f32[2048,128]{1,0:T(8,128)S(1)} %broadcast_select_fusion), channel_id=1, source_target_pairs={{0,2},{1,3},{2,0},{3,1},{4,6},{5,7},{6,4},{7,5},{8,10},{9,11},{10,... | collective-permute-start | bytes 3145736 | tf_op jit(solution)/shard_map/ppermute | solution.py:347
  157.9 17.3 %collective-permute-start.14 = (f32[544,128]{1,0:T(8,128)S(1)}, f32[544,128]{1,0:T(8,128)S(1)}, u32[]{:S(2)}, u32[]{:S(2)}) collective-permute-start(f32[544,128]{1,0:T(8,128)S(1)} %shard_map.138.dense_told), channel_id=1, source_target_pairs={{0,4},{1,5},{2,6},{3,7},{4,0},{5,1},{6,2},{7,3},{8,12},{9,13},{10,... | collective-permute-start | bytes 835592 | tf_op jit(solution)/shard_map/ppermute | solution.py:363
  159.4 15.8 %collective-permute-start.15 = (f32[544,128]{1,0:T(8,128)S(1)}, f32[544,128]{1,0:T(8,128)S(1)}, u32[]{:S(2)}, u32[]{:S(2)}) collective-permute-start(f32[544,128]{1,0:T(8,128)S(1)} %shard_map.139.pairs_told), channel_id=1, source_target_pairs={{0,4},{1,5},{2,6},{3,7},{4,0},{5,1},{6,2},{7,3},{8,12},{9,13},{10,... | collective-permute-start | bytes 835592 | tf_op jit(solution)/shard_map/ppermute | solution.py:363
  160.3 35.3 %collective-permute-start.9 = (f32[544,128]{1,0:T(8,128)S(1)}, f32[544,128]{1,0:T(8,128)S(1)}, u32[]{:S(2)}, u32[]{:S(2)}) collective-permute-start(f32[544,128]{1,0:T(8,128)S(1)} %shard_map.138.dense_told), channel_id=1, source_target_pairs={{0,6},{1,7},{2,4},{3,5},{4,2},{5,3},{6,0},{7,1},{8,14},{9,15},{10,... | collective-permute-start | bytes 835592 | tf_op jit(solution)/shard_map/ppermute | solution.py:363
  166.3 33.8 %collective-permute-start.13 = (f32[544,128]{1,0:T(8,128)S(1)}, f32[544,128]{1,0:T(8,128)S(1)}, u32[]{:S(2)}, u32[]{:S(2)}) collective-permute-start(f32[544,128]{1,0:T(8,128)S(1)} %shard_map.139.pairs_told), channel_id=1, source_target_pairs={{0,6},{1,7},{2,4},{3,5},{4,2},{5,3},{6,0},{7,1},{8,14},{9,15},{10,... | collective-permute-start | bytes 835592 | tf_op jit(solution)/shard_map/ppermute | solution.py:363
  203.3 0.7 copy-start.13
  203.3 4.5 %copy-start.8 = (s32[104,128]{1,0:T(8,128)S(1)}, s32[104,128]{1,0:T(8,128)}, u32[]{:S(2)}) copy-start(s32[104,128]{1,0:T(8,128)} %get-tuple-element.19.meta_s.meta_v) | copy-start | bytes 159748
  203.4 28.4 %collective-permute-start.18 = (f32[264,1024]{1,0:T(8,128)S(1)}, f32[264,1024]{1,0:T(8,128)S(1)}, u32[]{:S(2)}, u32[]{:S(2)}) collective-permute-start(f32[264,1024]{1,0:T(8,128)S(1)} %slice.18), channel_id=1, source_target_pairs={{0,1},{1,0},{2,3},{3,2},{4,5},{5,4},{6,7},{7,6},{8,9},{9,8},{10,11... | collective-permute-start | bytes 3244040 | tf_op jit(solution)/shard_map/ppermute | solution.py:363
  204.0 2.2 collective-permute-start.4
  206.2 23.3 %collective-permute-start.5 = (f32[16,128]{1,0:T(8,128)S(1)}, f32[16,128]{1,0:T(8,128)S(1)}, u32[]{:S(2)}, u32[]{:S(2)}) collective-permute-start(f32[16,128]{1,0:T(8,128)S(1)} %broadcast_select_fusion.4), channel_id=1, source_target_pairs={{0,2},{1,3},{2,0},{3,1},{4,6},{5,7},{6,4},{7,5},{8,10},{9,11},{10,... | collective-permute-start | bytes 24584 | tf_op jit(solution)/shard_map/ppermute | solution.py:347
  226.2 3.3 %copy-start.3 = (bf16[2048,2048]{1,0:T(8,128)(2,1)}, bf16[2048,2048]{1,0:T(8,128)(2,1)S(1)}, u32[]{:S(2)}) copy-start(bf16[2048,2048]{1,0:T(8,128)(2,1)S(1)} %count.1.counts) | copy-start | bytes 25165828
  230.1 1.2 collective-permute-start.19

commit v2 on v1

--- a/solution.py
+++ b/solution.py
@@ -525,10 +525,12 @@
         in_specs=[SMEM, VMEM, pl.BlockSpec((table_rows // chunks, bags), lambda i: (i, 0)), piece, VMEM],
         out_specs=(piece, pl.BlockSpec((table_rows // LANES, LANES), lambda i: (0, 0))),
         scratch_shapes=[pltpu.VMEM((bags, width), F32), pltpu.VMEM((bags, 2 * width), BF16)],
-        compiler_params=pltpu.CompilerParams(vmem_limit_bytes=56 << 20),
+        compiler_params=pltpu.CompilerParams(vmem_limit_bytes=24 << 20),
         name="update",
     )
-    new_table, new_state = update(places, in_vmem(came), counts, held_table, held_state)
+    new_table, new_state = update(
+        places, in_vmem(came), pltpu.with_memory_space_constraint(counts, pltpu.HBM), held_table, held_state
+    )
     return new_table, new_state.reshape(-1), top_grad, out_grad
 
 

time: 242 us -> 241 us (level)
    unnamed x28 -> x30, local copies, waits for them, and re-layouts: 8.58 us -> 8.58 us
  transfers between devices with their start and end apart: 23 -> 23, of which waited for: 12 -> 12; matrix products, arithmetic and copies ran while one was open for 3% -> 2% of each run, Pallas kernels for 17% -> 17%
where the time goes in v2:
time: 241 us
  waiting for transfers between devices  111 us (46%)
  Pallas kernels  60.9 us (25%)
  starting transfers between devices  53.3 us (22%)
  local copies, waits for them, and re-layouts  10.8 us (4%)
  other arithmetic  3.41 us (1%)
    ppermute x14, waiting for transfers between devices, swap(): return lax.ppermute(value, AXES, [(d, d ^ offset) for d in range(devices)])  62.7 us
    all_to_all x3, waiting for transfers between devices, exchange(): return lax.all_to_all(x, AXES, split_axis=0, concat_axis=0, tiled=True)  45.4 us
    ppermute x14, starting transfers between devices, swap(): return lax.ppermute(value, AXES, [(d, d ^ offset) for d in range(devices)])  33.5 us
    pallas_call x1, Pallas kernels, on_device(): pl.pallas_call(functools.partial(count_kernel, look_tiles, rows), out_sha...  18.4 us
    all_to_all x3, starting transfers between devices, exchange(): return lax.all_to_all(x, AXES, split_axis=0, concat_axis=0, tiled=True)  14.1 us
    pallas_call x4, Pallas kernels, on_device(): pl.pallas_call(top_kernel, out_shape=shape((inter + 8, hidden), F32), in_...  12.6 us
    pallas_call x1, Pallas kernels, on_device(): pl.pallas_call(functools.partial(pool_kernel, look_tiles, rows), out_shap...  9.47 us
    unnamed x30, local copies, waits for them, and re-layouts  8.58 us
  transfers between devices with their start and end apart: 23, of which 12 were waited for; matrix products, arithmetic and copies ran while one was open for 2% of the time, Pallas kernels for 17%

profile of v2, /device:TPU:0, one launch (start us, length us, event | category | flops | bytes accessed | tf_op | source)
XLA Modules:
  0.0 240.8 jit_solution(14395932958497392430)
XLA Ops:
  0.6 2.6 %prep.1 = (s32[104,128]{1,0:T(8,128)}, s32[32,128]{1,0:T(8,128)}, s32[32,128]{1,0:T(8,128)}, f32[136,128]{1,0:T(8,128)}) custom-call(s32[48,128]{1,0:T(8,128)} %bitcast.38, s32[16,128]{1,0:T(8,128)} %bitcast.42, s32[16,128]{1,0:T(8,128)} %bitcast.43, s32[16,128]{1,0:T(8,128)} %bitcast.44, f32[128,128]{1,0:T(8,128)} %dense.3, f32[1,128]{1,0:T(1,128)} %bitcast.45), custom_call_target="tpu_custom_call" | custom-call | tf_op jit(solution)/shard_map/prep/pallas_call | solution.py:402
  3.3 0.5 collective-permute-start
  4.9 0.8 broadcast_select_fusion.2
  5.7 2.8 %collective-permute-start.1 = (s32[104,128]{1,0:T(8,128)S(1)}, s32[104,128]{1,0:T(8,128)S(1)}, u32[]{:S(2)}, u32[]{:S(2)}) collective-permute-start(s32[104,128]{1,0:T(8,128)S(1)} %broadcast_select_fusion.2), channel_id=1, source_target_pairs={{0,2},{1,3},{2,0},{3,1},{4,6},{5,7},{6,4},{7,5},{8,10},{9,11},{10,... | collective-permute-start | bytes 159752 | tf_op jit(solution)/shard_map/ppermute | solution.py:347
  8.5 1.3 stack.7.clone
  9.8 4.2 %all-to-all-start = ((s32[32,2,128]{2,1,0:T(2,128)}), s32[32,2,128]{2,1,0:T(2,128)S(1)}, u32[]{:S(2)}, u32[]{:S(2)}) async-start(s32[32,2,128]{2,1,0:T(2,128)} %stack.7.clone), calls=%async_computation | async-start | bytes 65536 | tf_op jit(solution)/shard_map/all_to_all | solution.py:354
  14.0 0.6 broadcast_select_fusion.3.meta_s.meta_v
  14.7 9.5 %pool.1 = f32[4096,128]{1,0:T(8,128)} custom-call(s32[104,128]{1,0:T(8,128)} %broadcast_select_fusion.3.meta_s.meta_v, s32[104,128]{1,0:T(8,128)} %broadcast_select_fusion.3.meta_s.meta_v, f32[2048,128]{1,0:T(8,128)} %table.1), custom_call_target="tpu_custom_call" | custom-call | tf_op jit(solution)/shard_map/pool/pallas_call | solution.py:427
  24.1 5.8 %all-to-all-start.1 = ((f32[32,128,128]{2,1,0:T(8,128)}), f32[32,128,128]{2,1,0:T(8,128)S(1)}, u32[]{:S(2)}, u32[]{:S(2)}) async-start(f32[32,128,128]{2,1,0:T(8,128)} %bitcast.35), calls=%async_computation.1 | async-start | bytes 4194304 | tf_op jit(solution)/shard_map/all_to_all | solution.py:354
  30.3 1.2 copy-done
  31.5 1.2 copy-done.4
  32.7 0.7 slice_reduce_fusion
  33.4 45.3 %all-to-all-done.1 = f32[32,128,128]{2,1,0:T(8,128)S(1)} async-done(((f32[32,128,128]{2,1,0:T(8,128)}), f32[32,128,128]{2,1,0:T(8,128)S(1)}, u32[]{:S(2)}, u32[]{:S(2)}) %all-to-all-start.1) | async-done | bytes 2097184 | tf_op jit(solution)/shard_map/all_to_all | solution.py:354
  78.7 1.0 copy-done.7
  79.7 3.1 %gram.1 = (f32[2176,128]{1,0:T(8,128)S(1)}, f32[136,128]{1,0:T(8,128)S(1)}) custom-call(s32[32,128]{1,0:T(8,128)S(1)} %bitcast.28, s32[32]{0:T(128)S(1)} %iota_xor_fusion.source, f32[4096,128]{1,0:T(8,128)S(1)} %bitcast.27, f32[128,128]{1,0:T(8,128)S(1)} %copy-done.7), custom_call_target="tpu_custom_call" | custom-call | tf_op jit(solution)/shard_map/gram/pallas_call | solution.py:468
  82.9 1.4 copy-done.5
  84.3 6.1 %back.1 = f32[4096,128]{1,0:T(8,128)} custom-call(s32[32,128]{1,0:T(8,128)} %bitcast.29, f32[128,128]{1,0:T(8,128)} %dense.3, f32[2176,128]{1,0:T(8,128)S(1)} %get-tuple-element.21.turned, f32[136,128]{1,0:T(8,128)S(1)} %get-tuple-element.22.pairs.refs_0_, f32[1,128]{1,0:T(1,128)} %bitcast.46, bf16[896,1024]{1,0:T(8,128)(2,1)S(1)} %copy-done.1, ...), custom_call_target="tpu_custom_call" | custom-call | tf_op jit(solution)/shard_map/back/pallas_call | solution.py:480
  90.4 4.1 %all-to-all-start.2 = ((f32[32,128,128]{2,1,0:T(8,128)}), f32[32,128,128]{2,1,0:T(8,128)S(1)}, u32[]{:S(2)}, u32[]{:S(2)}) async-start(f32[32,128,128]{2,1,0:T(8,128)} %bitcast.36), calls=%async_computation.2 | async-start | bytes 4194304 | tf_op jit(solution)/shard_map/all_to_all | solution.py:354
  94.8 3.5 %collective-permute-start.8 = (f32[136,128]{1,0:T(8,128)S(1)}, f32[136,128]{1,0:T(8,128)S(1)}, u32[]{:S(2)}, u32[]{:S(2)}) collective-permute-start(f32[136,128]{1,0:T(8,128)S(1)} %copy-done.11), channel_id=1, source_target_pairs={{0,24},{1,25},{2,26},{3,27},{4,28},{5,29},{6,30},{7,31},{8,16},{9,... | collective-permute-start | bytes 208904 | tf_op jit(solution)/shard_map/ppermute | solution.py:363
  98.3 0.9 collective-permute-start.6
  99.2 3.5 %collective-permute-start.12 = (f32[136,128]{1,0:T(8,128)S(1)}, f32[136,128]{1,0:T(8,128)S(1)}, u32[]{:S(2)}, u32[]{:S(2)}) collective-permute-start(f32[136,128]{1,0:T(8,128)S(1)} %get-tuple-element.22.pairs.refs_0_), channel_id=1, source_target_pairs={{0,24},{1,25},{2,26},{3,27},{4,28},{5,29},{6,30},{7,31},{8,16},{9,... | collective-permute-start | bytes 208904 | tf_op jit(solution)/shard_map/ppermute | solution.py:363
  102.7 32.3 %collective-permute-done.8.refs_3_ = f32[136,128]{1,0:T(8,128)S(1)} collective-permute-done((f32[136,128]{1,0:T(8,128)S(1)}, f32[136,128]{1,0:T(8,128)S(1)}, u32[]{:S(2)}, u32[]{:S(2)}) %collective-permute-start.8) | collective-permute-done | bytes 69664 | tf_op jit(solution)/shard_map/ppermute | solution.py:363
  135.0 15.2 %collective-permute-start.11 = (f32[136,128]{1,0:T(8,128)S(1)}, f32[136,128]{1,0:T(8,128)S(1)}, u32[]{:S(2)}, u32[]{:S(2)}) collective-permute-start(f32[136,128]{1,0:T(8,128)S(1)} %get-tuple-element.22.pairs.refs_0_), channel_id=1, source_target_pairs={{0,16},{1,17},{2,18},{3,19},{4,20},{5,21},{6,22},{7,23},{8,24},{9,... | collective-permute-start | bytes 208904 | tf_op jit(solution)/shard_map/ppermute | solution.py:363
  150.2 1.0 collective-permute-done.7.refs_2_
  151.3 1.6 collective-permute-start.16
  152.9 2.3 collective-permute-done.11.refs_2_
  155.7 1.6 collective-permute-start.17
  157.5 0.5 collective-permute-start.3
  158.0 1.4 collective-permute-start.14
  159.4 0.6 collective-permute-start.15
  160.4 2.4 %collective-permute-start.9 = (f32[544,128]{1,0:T(8,128)S(1)}, f32[544,128]{1,0:T(8,128)S(1)}, u32[]{:S(2)}, u32[]{:S(2)}) collective-permute-start(f32[544,128]{1,0:T(8,128)S(1)} %shard_map.138.dense_told), channel_id=1, source_target_pairs={{0,6},{1,7},{2,4},{3,5},{4,2},{5,3},{6,0},{7,1},{8,14},{9,15},{10,... | collective-permute-start | bytes 835592 | tf_op jit(solution)/shard_map/ppermute | solution.py:363
  162.8 3.5 %collective-permute-done.17.pairs_told = f32[544,128]{1,0:T(8,128)S(1)} collective-permute-done((f32[544,128]{1,0:T(8,128)S(1)}, f32[544,128]{1,0:T(8,128)S(1)}, u32[]{:S(2)}, u32[]{:S(2)}) %collective-permute-start.17) | collective-permute-done | bytes 278560 | tf_op jit(solution)/shard_map/ppermute | solution.py:363
  166.3 2.4 %collective-permute-start.13 = (f32[544,128]{1,0:T(8,128)S(1)}, f32[544,128]{1,0:T(8,128)S(1)}, u32[]{:S(2)}, u32[]{:S(2)}) collective-permute-start(f32[544,128]{1,0:T(8,128)S(1)} %shard_map.139.pairs_told), channel_id=1, source_target_pairs={{0,6},{1,7},{2,4},{3,5},{4,2},{5,3},{6,0},{7,1},{8,14},{9,15},{10,... | collective-permute-start | bytes 835592 | tf_op jit(solution)/shard_map/ppermute | solution.py:363
  168.9 3.1 %top.4.before = f32[272,1024]{1,0:T(8,128)S(1)} custom-call(f32[544,128]{1,0:T(8,128)S(1)} %shard_map.138.dense_told, f32[544,128]{1,0:T(8,128)S(1)} %shard_map.139.pairs_told, bf16[896,1024]{1,0:T(8,128)(2,1)S(1)} %copy-done.2, f32[1,1024]{1,0:T(1,128)S(1)} %bitcast.31, f32[272,1024]{1,0:T(8,128)S(1)} %broadcast_in_dim.3.before), custom_call_target="tpu_custom_call" | custom-call | tf_op jit(solution)/shard_map/top/pallas_call | solution.py:509
  172.1 3.2 %top.5.before = f32[272,1024]{1,0:T(8,128)S(1)} custom-call(f32[544,128]{1,0:T(8,128)S(1)} %collective-permute-done.16.dense_told, f32[544,128]{1,0:T(8,128)S(1)} %collective-permute-done.17.pairs_told, bf16[896,1024]{1,0:T(8,128)(2,1)S(1)} %copy-done.2, f32[1,1024]{1,0:T(1,128)S(1)} %bitcast.32, f32[272,1024]{1,0:T(8,128)S(1)} %top.4.before), custom_call_target="tpu_custom_call" | custom-call | tf_op jit(solution)/shard_map/top/pallas_call | solution.py:509
  175.3 3.1 %top.6.before = f32[272,1024]{1,0:T(8,128)S(1)} custom-call(f32[544,128]{1,0:T(8,128)S(1)} %collective-permute-done.14.dense_told, f32[544,128]{1,0:T(8,128)S(1)} %collective-permute-done.15.pairs_told, bf16[896,1024]{1,0:T(8,128)(2,1)S(1)} %copy-done.2, f32[1,1024]{1,0:T(1,128)S(1)} %bitcast.33, f32[272,1024]{1,0:T(8,128)S(1)} %top.5.before), custom_call_target="tpu_custom_call" | custom-call | tf_op jit(solution)/shard_map/top/pallas_call | solution.py:509
  178.4 17.3 %collective-permute-done.9.dense_told = f32[544,128]{1,0:T(8,128)S(1)} collective-permute-done((f32[544,128]{1,0:T(8,128)S(1)}, f32[544,128]{1,0:T(8,128)S(1)}, u32[]{:S(2)}, u32[]{:S(2)}) %collective-permute-start.9) | collective-permute-done | bytes 278560 | tf_op jit(solution)/shard_map/ppermute | solution.py:363
  195.6 4.5 %collective-permute-done.13.pairs_told = f32[544,128]{1,0:T(8,128)S(1)} collective-permute-done((f32[544,128]{1,0:T(8,128)S(1)}, f32[544,128]{1,0:T(8,128)S(1)}, u32[]{:S(2)}, u32[]{:S(2)}) %collective-permute-start.13) | collective-permute-done | bytes 278560 | tf_op jit(solution)/shard_map/ppermute | solution.py:363
  200.1 3.1 %top.7 = f32[272,1024]{1,0:T(8,128)S(1)} custom-call(f32[544,128]{1,0:T(8,128)S(1)} %collective-permute-done.9.dense_told, f32[544,128]{1,0:T(8,128)S(1)} %collective-permute-done.13.pairs_told, bf16[896,1024]{1,0:T(8,128)(2,1)S(1)} %copy-done.2, f32[1,1024]{1,0:T(1,128)S(1)} %bitcast.34, f32[272,1024]{1,0:T(8,128)S(1)} %top.6.before), custom_call_target="tpu_custom_call" | custom-call | tf_op jit(solution)/shard_map/top/pallas_call | solution.py:509
  203.5 0.5 copy-done.14
  204.0 2.2 collective-permute-done.4
  206.2 1.6 collective-permute-start.5
  207.8 18.4 %count.1.counts = bf16[2048,2048]{1,0:T(8,128)(2,1)S(1)} custom-call(s32[104,128]{1,0:T(8,128)S(1)} %copy-done.8, s32[104,128]{1,0:T(8,128)S(1)} %copy-done.8), custom_call_target="tpu_custom_call" | custom-call | tf_op jit(solution)/shard_map/count/pallas_call | solution.py:447
  226.2 3.3 %copy-done.3 = bf16[2048,2048]{1,0:T(8,128)(2,1)} copy-done((bf16[2048,2048]{1,0:T(8,128)(2,1)}, bf16[2048,2048]{1,0:T(8,128)(2,1)S(1)}, u32[]{:S(2)}) %copy-start.3) | copy-done | bytes 8388632
  229.7 1.0 collective-permute-done.19
  230.7 0.6 add.9
  231.3 1.1 slice_add_fusion
  232.5 8.3 %update.1 = (f32[2048,128]{1,0:T(8,128)}, f32[16,128]{1,0:T(8,128)}) custom-call(s32[32,128]{1,0:T(8,128)S(1)} %copy-done.12, f32[4096,128]{1,0:T(8,128)S(1)} %bitcast.26, bf16[2048,2048]{1,0:T(8,128)(2,1)} %copy-done.3, f32[2048,128]{1,0:T(8,128)S(1)} %broadcast_select_fusion.1.table, f32[16,128]{1,0:T(8,128)S(1)} %broadcast_select_fusion.5.state), custom_call_target="tpu_custom_call" | custom-call | tf_op jit(solution)/shard_map/update/pallas_call | solution.py:531
  (56 shorter events, 2.5 us)
Async XLA Ops:
  3.3 1.6 collective-permute-start
  5.7 8.4 %collective-permute-start.1 = (s32[104,128]{1,0:T(8,128)S(1)}, s32[104,128]{1,0:T(8,128)S(1)}, u32[]{:S(2)}, u32[]{:S(2)}) collective-permute-start(s32[104,128]{1,0:T(8,128)S(1)} %broadcast_select_fusion.2), channel_id=1, source_target_pairs={{0,2},{1,3},{2,0},{3,1},{4,6},{5,7},{6,4},{7,5},{8,10},{9,11},{10,... | collective-permute-start | bytes 159752 | tf_op jit(solution)/shard_map/ppermute | solution.py:347
  9.8 14.3 %all-to-all-start = ((s32[32,2,128]{2,1,0:T(2,128)}), s32[32,2,128]{2,1,0:T(2,128)S(1)}, u32[]{:S(2)}, u32[]{:S(2)}) async-start(s32[32,2,128]{2,1,0:T(2,128)} %stack.7.clone), calls=%async_computation | async-start | bytes 65536 | tf_op jit(solution)/shard_map/all_to_all | solution.py:354
  24.1 5.8 %copy-start.6 = (f32[264,1024]{1,0:T(8,128)S(1)}, f32[264,1024]{1,0:T(8,128)}, u32[]{:S(2)}) copy-start(f32[264,1024]{1,0:T(8,128)} %weight.1) | copy-start | bytes 3244036
  24.1 54.6 %all-to-all-start.1 = ((f32[32,128,128]{2,1,0:T(8,128)}), f32[32,128,128]{2,1,0:T(8,128)S(1)}, u32[]{:S(2)}, u32[]{:S(2)}) async-start(f32[32,128,128]{2,1,0:T(8,128)} %bitcast.35), calls=%async_computation.1 | async-start | bytes 4194304 | tf_op jit(solution)/shard_map/all_to_all | solution.py:354
  30.3 1.2 copy-start
  31.5 1.2 copy-start.4
  32.7 50.1 %copy-start.9 = (s32[32,1,128]{2,1,0:T(1,128)}, s32[32,1,128]{2,1,0:T(1,128)S(1)}, u32[]{:S(2)}) copy-start(s32[32,1,128]{2,1,0:T(1,128)S(1)} %slice.16) | copy-start | bytes 49156
  78.7 4.1 %copy-start.1 = (bf16[896,1024]{1,0:T(8,128)(2,1)S(1)}, bf16[896,1024]{1,0:T(8,128)(2,1)}, u32[]{:S(2)}) copy-start(bf16[896,1024]{1,0:T(8,128)(2,1)} %copy-done) | copy-start | bytes 5505028
  78.7 1.0 copy-start.7
  82.9 1.4 copy-start.5
  90.4 4.4 %copy-start.11 = (f32[136,128]{1,0:T(8,128)S(1)}, f32[136,128]{1,0:T(8,128)}, u32[]{:S(2)}) copy-start(f32[136,128]{1,0:T(8,128)} %get-tuple-element.27.refs_0_) | copy-start | bytes 208900
  90.4 142.1 %all-to-all-start.2 = ((f32[32,128,128]{2,1,0:T(8,128)}), f32[32,128,128]{2,1,0:T(8,128)S(1)}, u32[]{:S(2)}, u32[]{:S(2)}) async-start(f32[32,128,128]{2,1,0:T(8,128)} %bitcast.36), calls=%async_computation.2 | async-start | bytes 4194304 | tf_op jit(solution)/shard_map/all_to_all | solution.py:354
  94.5 62.8 %copy-start.13 = (f32[2048,128]{1,0:T(8,128)S(1)}, f32[2048,128]{1,0:T(8,128)}, u32[]{:S(2)}) copy-start(f32[2048,128]{1,0:T(8,128)} %table.1) | copy-start | bytes 3145732
  94.5 62.8 %collective-permute-start.2 = (f32[2048,128]{1,0:T(8,128)}, f32[2048,128]{1,0:T(8,128)S(1)}, u32[]{:S(2)}, u32[]{:S(2)}) collective-permute-start(f32[2048,128]{1,0:T(8,128)} %table.1), channel_id=1, source_target_pairs={{0,1},{1,0},{2,3},{3,2},{4,5},{5,4},{6,7},{7,6},{8,9},{9,8},{10,11... | collective-permute-start | bytes 3145736 | tf_op jit(solution)/shard_map/ppermute | solution.py:347
  94.8 40.2 %collective-permute-start.8 = (f32[136,128]{1,0:T(8,128)S(1)}, f32[136,128]{1,0:T(8,128)S(1)}, u32[]{:S(2)}, u32[]{:S(2)}) collective-permute-start(f32[136,128]{1,0:T(8,128)S(1)} %copy-done.11), channel_id=1, source_target_pairs={{0,24},{1,25},{2,26},{3,27},{4,28},{5,29},{6,30},{7,31},{8,16},{9,... | collective-permute-start | bytes 208904 | tf_op jit(solution)/shard_map/ppermute | solution.py:363
  98.3 52.9 %collective-permute-start.7 = (f32[136,128]{1,0:T(8,128)S(1)}, f32[136,128]{1,0:T(8,128)S(1)}, u32[]{:S(2)}, u32[]{:S(2)}) collective-permute-start(f32[136,128]{1,0:T(8,128)S(1)} %copy-done.11), channel_id=1, source_target_pairs={{0,16},{1,17},{2,18},{3,19},{4,20},{5,21},{6,22},{7,23},{8,24},{9,... | collective-permute-start | bytes 208904 | tf_op jit(solution)/shard_map/ppermute | solution.py:363
  98.3 52.9 %collective-permute-start.6 = (f32[136,128]{1,0:T(8,128)S(1)}, f32[136,128]{1,0:T(8,128)S(1)}, u32[]{:S(2)}, u32[]{:S(2)}) collective-permute-start(f32[136,128]{1,0:T(8,128)S(1)} %copy-done.11), channel_id=1, source_target_pairs={{0,8},{1,9},{2,10},{3,11},{4,12},{5,13},{6,14},{7,15},{8,0},{9,1},... | collective-permute-start | bytes 208904 | tf_op jit(solution)/shard_map/ppermute | solution.py:363
  99.2 53.7 %collective-permute-start.12 = (f32[136,128]{1,0:T(8,128)S(1)}, f32[136,128]{1,0:T(8,128)S(1)}, u32[]{:S(2)}, u32[]{:S(2)}) collective-permute-start(f32[136,128]{1,0:T(8,128)S(1)} %get-tuple-element.22.pairs.refs_0_), channel_id=1, source_target_pairs={{0,24},{1,25},{2,26},{3,27},{4,28},{5,29},{6,30},{7,31},{8,16},{9,... | collective-permute-start | bytes 208904 | tf_op jit(solution)/shard_map/ppermute | solution.py:363
  135.0 20.3 %collective-permute-start.11 = (f32[136,128]{1,0:T(8,128)S(1)}, f32[136,128]{1,0:T(8,128)S(1)}, u32[]{:S(2)}, u32[]{:S(2)}) collective-permute-start(f32[136,128]{1,0:T(8,128)S(1)} %get-tuple-element.22.pairs.refs_0_), channel_id=1, source_target_pairs={{0,16},{1,17},{2,18},{3,19},{4,20},{5,21},{6,22},{7,23},{8,24},{9,... | collective-permute-start | bytes 208904 | tf_op jit(solution)/shard_map/ppermute | solution.py:363
  151.3 4.4 %collective-permute-start.10 = (f32[136,128]{1,0:T(8,128)S(1)}, f32[136,128]{1,0:T(8,128)S(1)}, u32[]{:S(2)}, u32[]{:S(2)}) collective-permute-start(f32[136,128]{1,0:T(8,128)S(1)} %get-tuple-element.22.pairs.refs_0_), channel_id=1, source_target_pairs={{0,8},{1,9},{2,10},{3,11},{4,12},{5,13},{6,14},{7,15},{8,0},{9,1},... | collective-permute-start | bytes 208904 | tf_op jit(solution)/shard_map/ppermute | solution.py:363
  151.3 9.1 %collective-permute-start.16 = (f32[544,128]{1,0:T(8,128)S(1)}, f32[544,128]{1,0:T(8,128)S(1)}, u32[]{:S(2)}, u32[]{:S(2)}) collective-permute-start(f32[544,128]{1,0:T(8,128)S(1)} %shard_map.138.dense_told), channel_id=1, source_target_pairs={{0,2},{1,3},{2,0},{3,1},{4,6},{5,7},{6,4},{7,5},{8,10},{9,11},{10,... | collective-permute-start | bytes 835592 | tf_op jit(solution)/shard_map/ppermute | solution.py:363
  155.7 10.7 %collective-permute-start.17 = (f32[544,128]{1,0:T(8,128)S(1)}, f32[544,128]{1,0:T(8,128)S(1)}, u32[]{:S(2)}, u32[]{:S(2)}) collective-permute-start(f32[544,128]{1,0:T(8,128)S(1)} %shard_map.139.pairs_told), channel_id=1, source_target_pairs={{0,2},{1,3},{2,0},{3,1},{4,6},{5,7},{6,4},{7,5},{8,10},{9,11},{10,... | collective-permute-start | bytes 835592 | tf_op jit(solution)/shard_map/ppermute | solution.py:363
  157.3 11.6 %copy-start.2 = (bf16[896,1024]{1,0:T(8,128)(2,1)S(1)}, bf16[896,1024]{1,0:T(8,128)(2,1)}, u32[]{:S(2)}) copy-start(bf16[896,1024]{1,0:T(8,128)(2,1)} %copy-done) | copy-start | bytes 5505028
  157.4 11.5 %copy-start.10 = (f32[1024]{0:T(1024)S(1)}, f32[1024]{0:T(1024)}, u32[]{:S(2)}) copy-start(f32[1024]{0:T(1024)} %param.21) | copy-start | bytes 12292
  157.5 72.1 %collective-permute-start.3 = (f32[2048,128]{1,0:T(8,128)S(1)}, f32[2048,128]{1,0:T(8,128)S(1)}, u32[]{:S(2)}, u32[]{:S(2)}) collective-permute-start(f32[2048,128]{1,0:T(8,128)S(1)} %broadcast_select_fusion), channel_id=1, source_target_pairs={{0,2},{1,3},{2,0},{3,1},{4,6},{5,7},{6,4},{7,5},{8,10},{9,11},{10,... | collective-permute-start | bytes 3145736 | tf_op jit(solution)/shard_map/ppermute | solution.py:347
  158.0 17.3 %collective-permute-start.14 = (f32[544,128]{1,0:T(8,128)S(1)}, f32[544,128]{1,0:T(8,128)S(1)}, u32[]{:S(2)}, u32[]{:S(2)}) collective-permute-start(f32[544,128]{1,0:T(8,128)S(1)} %shard_map.138.dense_told), channel_id=1, source_target_pairs={{0,4},{1,5},{2,6},{3,7},{4,0},{5,1},{6,2},{7,3},{8,12},{9,13},{10,... | collective-permute-start | bytes 835592 | tf_op jit(solution)/shard_map/ppermute | solution.py:363
  159.4 15.8 %collective-permute-start.15 = (f32[544,128]{1,0:T(8,128)S(1)}, f32[544,128]{1,0:T(8,128)S(1)}, u32[]{:S(2)}, u32[]{:S(2)}) collective-permute-start(f32[544,128]{1,0:T(8,128)S(1)} %shard_map.139.pairs_told), channel_id=1, source_target_pairs={{0,4},{1,5},{2,6},{3,7},{4,0},{5,1},{6,2},{7,3},{8,12},{9,13},{10,... | collective-permute-start | bytes 835592 | tf_op jit(solution)/shard_map/ppermute | solution.py:363
  160.4 35.3 %collective-permute-start.9 = (f32[544,128]{1,0:T(8,128)S(1)}, f32[544,128]{1,0:T(8,128)S(1)}, u32[]{:S(2)}, u32[]{:S(2)}) collective-permute-start(f32[544,128]{1,0:T(8,128)S(1)} %shard_map.138.dense_told), channel_id=1, source_target_pairs={{0,6},{1,7},{2,4},{3,5},{4,2},{5,3},{6,0},{7,1},{8,14},{9,15},{10,... | collective-permute-start | bytes 835592 | tf_op jit(solution)/shard_map/ppermute | solution.py:363
  166.3 33.8 %collective-permute-start.13 = (f32[544,128]{1,0:T(8,128)S(1)}, f32[544,128]{1,0:T(8,128)S(1)}, u32[]{:S(2)}, u32[]{:S(2)}) collective-permute-start(f32[544,128]{1,0:T(8,128)S(1)} %shard_map.139.pairs_told), channel_id=1, source_target_pairs={{0,6},{1,7},{2,4},{3,5},{4,2},{5,3},{6,0},{7,1},{8,14},{9,15},{10,... | collective-permute-start | bytes 835592 | tf_op jit(solution)/shard_map/ppermute | solution.py:363
  203.3 0.7 copy-start.14
  203.3 4.5 %copy-start.8 = (s32[104,128]{1,0:T(8,128)S(1)}, s32[104,128]{1,0:T(8,128)}, u32[]{:S(2)}) copy-start(s32[104,128]{1,0:T(8,128)} %get-tuple-element.19.meta_s.meta_v) | copy-start | bytes 159748
  203.4 27.9 %collective-permute-start.18 = (f32[264,1024]{1,0:T(8,128)S(1)}, f32[264,1024]{1,0:T(8,128)S(1)}, u32[]{:S(2)}, u32[]{:S(2)}) collective-permute-start(f32[264,1024]{1,0:T(8,128)S(1)} %slice.18), channel_id=1, source_target_pairs={{0,1},{1,0},{2,3},{3,2},{4,5},{5,4},{6,7},{7,6},{8,9},{9,8},{10,11... | collective-permute-start | bytes 3244040 | tf_op jit(solution)/shard_map/ppermute | solution.py:363
  204.0 2.2 collective-permute-start.4
  206.2 23.3 %collective-permute-start.5 = (f32[16,128]{1,0:T(8,128)S(1)}, f32[16,128]{1,0:T(8,128)S(1)}, u32[]{:S(2)}, u32[]{:S(2)}) collective-permute-start(f32[16,128]{1,0:T(8,128)S(1)} %broadcast_select_fusion.4), channel_id=1, source_target_pairs={{0,2},{1,3},{2,0},{3,1},{4,6},{5,7},{6,4},{7,5},{8,10},{9,11},{10,... | collective-permute-start | bytes 24584 | tf_op jit(solution)/shard_map/ppermute | solution.py:347
  226.2 3.3 %copy-start.3 = (bf16[2048,2048]{1,0:T(8,128)(2,1)}, bf16[2048,2048]{1,0:T(8,128)(2,1)S(1)}, u32[]{:S(2)}) copy-start(bf16[2048,2048]{1,0:T(8,128)(2,1)S(1)} %count.1.counts) | copy-start | bytes 25165828
  229.5 1.2 collective-permute-start.19
  231.3 1.1 copy-start.12
